TPU v7x, 32 devices: a whole 2x2x4 slice. The times are simulated.
32 devices in a mesh: dp: 8 (over z, y), tensor: 4 (over x, core).
Axes of the slice: x: 2, y: 2, z: 4, core: 2. Of those that a mesh axis runs over, the one named last changes fastest.
Arguments:
- inputs: bfloat16 [16, 1024, 512], P('dp', 'tensor'), may hold values from -6 to 6
- memory: bfloat16 [16, 1024, 512], P('dp', 'tensor'), may hold values from -6 to 6
- tgt_len: int32 [16], P('dp'), may hold values from 512 to 1024, as said below
- src_len: int32 [16], P('dp'), may hold values from 512 to 1024, as said below
- cotangent: bfloat16 [16, 1024, 512], P('dp', 'tensor'), may hold values from -6 to 6
- w_qkv: bfloat16 [3, 512, 512], P(None, 'dp', 'tensor'), may hold values from -0.25 to 0.25
- w_out: bfloat16 [512, 512], P('tensor', 'dp'), may hold values from -6 to 6
- cross_query: bfloat16 [512, 512], P('dp', 'tensor'), may hold values from -0.25 to 0.25
- cross_kv: bfloat16 [2, 512, 512], P(None, 'dp', 'tensor'), may hold values from -0.25 to 0.25
- cross_out: bfloat16 [512, 512], P('tensor', 'dp'), may hold values from -6 to 6
- ffn_up: bfloat16 [512, 2048], P('dp', 'tensor'), may hold values from -0.25 to 0.25
- ffn_down: bfloat16 [2048, 512], P('tensor', 'dp'), may hold values from -0.1875 to 0.1875
- gain_one: bfloat16 [512], P('dp'), may hold values from 0.099609375 to 1.8984375
- bias_one: bfloat16 [512], P('dp'), may hold values from -3 to 3
- gain_two: bfloat16 [512], P('dp'), may hold values from 0.099609375 to 1.8984375
- bias_two: bfloat16 [512], P('dp'), may hold values from -3 to 3
- gain_three: bfloat16 [512], P('dp'), may hold values from 0.099609375 to 1.8984375
- bias_three: bfloat16 [512], P('dp'), may hold values from -3 to 3
Outputs:
- output: bfloat16 [16, 1024, 512], P('dp', 'tensor')
- grad_inputs: float32 [16, 1024, 512], P('dp', 'tensor')
- grad_memory: float32 [16, 1024, 512], P('dp', 'tensor')
- grad_w_qkv: float32 [3, 512, 512], P(None, 'dp', 'tensor')
- grad_w_out: float32 [512, 512], P('tensor', 'dp')
- grad_cross_query: float32 [512, 512], P('dp', 'tensor')
- grad_cross_kv: float32 [2, 512, 512], P(None, 'dp', 'tensor')
- grad_cross_out: float32 [512, 512], P('tensor', 'dp')
- grad_ffn_up: float32 [512, 2048], P('dp', 'tensor')
- grad_ffn_down: float32 [2048, 512], P('tensor', 'dp')
- grad_gain_one: float32 [512], P('dp')
- grad_bias_one: float32 [512], P('dp')
- grad_gain_two: float32 [512], P('dp')
- grad_bias_two: float32 [512], P('dp')
- grad_gain_three: float32 [512], P('dp')
- grad_bias_three: float32 [512], P('dp')
Inputs may be any that keep to these rules, and one draw needn't show every extreme that they name: `tgt_len`: one sequence has a target length of 1024 and another of 512. `src_len`: one sequence has a source length of 1024 and another of 512.
All inputs are finite; a program needn't handle non-finite values.
Results may differ from a plain program's by a relative error of at most 0.015.
Values may be sent and summed in bfloat16 or wider, within the bound.
A program may use at most 128 MiB of HBM per device.

v0:
```python
import jax
import jax.numpy as jnp
from jax import lax
from jax.sharding import PartitionSpec as P

DH = 64


EPSILON = 1e-05
MASKED = -1e30
BLOCK_ROWS = 512


def layer_norm(values, gain_vec, bias_vec):
    center = values - jnp.mean(values, axis=-1, keepdims=True)
    spread = jnp.mean(center * center, axis=-1, keepdims=True)
    return center * lax.rsqrt(spread + EPSILON) * gain_vec + bias_vec


def smooth_gate(values):
    return jax.nn.gelu(values, approximate=True)


def gather_weights(
    w_qkv,
    w_out,
    cross_query,
    cross_kv,
    cross_out,
    ffn_up,
    ffn_down,
    gain_one,
    bias_one,
    gain_two,
    bias_two,
    gain_three,
    bias_three,
):
    return (
        lax.all_gather(w_qkv, "dp", axis=1, tiled=True),
        lax.all_gather(w_out, "dp", axis=1, tiled=True),
        lax.all_gather(cross_query, "dp", axis=0, tiled=True),
        lax.all_gather(cross_kv, "dp", axis=1, tiled=True),
        lax.all_gather(cross_out, "dp", axis=1, tiled=True),
        lax.all_gather(ffn_up, "dp", axis=0, tiled=True),
        lax.all_gather(ffn_down, "dp", axis=1, tiled=True),
        lax.all_gather(gain_one, "dp", axis=0, tiled=True),
        lax.all_gather(bias_one, "dp", axis=0, tiled=True),
        lax.all_gather(gain_two, "dp", axis=0, tiled=True),
        lax.all_gather(bias_two, "dp", axis=0, tiled=True),
        lax.all_gather(gain_three, "dp", axis=0, tiled=True),
        lax.all_gather(bias_three, "dp", axis=0, tiled=True),
    )


def reduce_grads(
    grad_qkv,
    grad_out,
    grad_query,
    grad_pair,
    grad_cross,
    grad_up,
    grad_down,
    grad_gain_one,
    grad_bias_one,
    grad_gain_two,
    grad_bias_two,
    grad_gain_three,
    grad_bias_three,
):
    return (
        lax.psum_scatter(grad_qkv, "dp", scatter_dimension=1, tiled=True),
        lax.psum_scatter(grad_out, "dp", scatter_dimension=1, tiled=True),
        lax.psum_scatter(grad_query, "dp", scatter_dimension=0, tiled=True),
        lax.psum_scatter(grad_pair, "dp", scatter_dimension=1, tiled=True),
        lax.psum_scatter(grad_cross, "dp", scatter_dimension=1, tiled=True),
        lax.psum_scatter(grad_up, "dp", scatter_dimension=0, tiled=True),
        lax.psum_scatter(grad_down, "dp", scatter_dimension=1, tiled=True),
        lax.psum_scatter(grad_gain_one, "dp", scatter_dimension=0, tiled=True),
        lax.psum_scatter(grad_bias_one, "dp", scatter_dimension=0, tiled=True),
        lax.psum_scatter(grad_gain_two, "dp", scatter_dimension=0, tiled=True),
        lax.psum_scatter(grad_bias_two, "dp", scatter_dimension=0, tiled=True),
        lax.psum_scatter(grad_gain_three, "dp", scatter_dimension=0, tiled=True),
        lax.psum_scatter(grad_bias_three, "dp", scatter_dimension=0, tiled=True),
    )


def norm_rows(own_part):
    return lax.all_gather(own_part, "tensor", axis=0, tiled=True)


def grad_rows(own_part):
    return lax.all_gather(own_part, "tensor", axis=0, tiled=True)


def branch_sum(mixture, weight):
    return lax.psum_scatter(
        jnp.dot(mixture, weight, preferred_element_type=jnp.float32),
        "tensor",
        scatter_dimension=0,
        tiled=True,
    )


def input_grad(grad_term, own_rows):
    return lax.psum_scatter(
        grad_term(jnp.int32(0), own_rows * lax.axis_size("tensor")),
        "tensor",
        scatter_dimension=0,
        tiled=True,
    )


def head_view(matrix):
    return matrix.reshape(matrix.shape[0], -1, DH)


def block_scores(query_block, key_heads, first_row, causal, length):
    scores = jnp.einsum("qhd,khd->hqk", query_block, key_heads, preferred_element_type=jnp.float32)
    scores = scores * DH ** (-0.5)
    row_ids = first_row + jnp.arange(query_block.shape[0])
    col_ids = jnp.arange(key_heads.shape[0])
    live_mask = col_ids[None, :] < length
    if causal:
        live_mask = live_mask & (col_ids[None, :] <= row_ids[:, None])
    return jnp.where(live_mask[None], scores, MASKED)


def attend_forward(queries, key_rows, value_rows, causal, length):
    row_total = queries.shape[0]
    block_size = min(BLOCK_ROWS, row_total)
    blocks = row_total // block_size
    query_heads = head_view(queries).reshape(blocks, block_size, -1, DH)
    key_heads = head_view(key_rows)
    value_heads = head_view(value_rows)

    def one_block(members):
        query_block, block_index = members
        scores = block_scores(query_block, key_heads, block_index * block_size, causal, length)
        row_max = jnp.max(scores, axis=-1, keepdims=True)
        shifted = jnp.exp(scores - row_max)
        summed = jnp.sum(shifted, axis=-1, keepdims=True)
        weights = (shifted / summed).astype(jnp.bfloat16)
        mixture = jnp.einsum(
            "hqk,khd->qhd", weights, value_heads, preferred_element_type=jnp.float32
        )
        return (mixture.astype(jnp.bfloat16), (row_max + jnp.log(summed))[..., 0])

    mixture, log_norm = lax.map(one_block, (query_heads, jnp.arange(blocks)))
    return (mixture.reshape(row_total, -1), log_norm)


def attend_backward(queries, key_rows, value_rows, grad_mix, log_norm, causal, length):
    row_total = queries.shape[0]
    block_size = min(BLOCK_ROWS, row_total)
    blocks = row_total // block_size
    query_heads = head_view(queries).reshape(blocks, block_size, -1, DH)
    grad_heads = head_view(grad_mix).reshape(blocks, block_size, -1, DH)
    key_heads = head_view(key_rows)
    value_heads = head_view(value_rows)
    scale_value = DH ** (-0.5)

    def one_block(carry, members):
        query_block, grad_block, norm_block, block_index = members
        scores = block_scores(query_block, key_heads, block_index * block_size, causal, length)
        probs = jnp.exp(scores - norm_block[..., None])
        grad_probs = jnp.einsum(
            "qhd,khd->hqk", grad_block, value_heads, preferred_element_type=jnp.float32
        )
        inner = jnp.sum(probs * grad_probs, axis=-1, keepdims=True)
        grad_scores = (probs * (grad_probs - inner)).astype(jnp.bfloat16)
        grad_query = (
            jnp.einsum("hqk,khd->qhd", grad_scores, key_heads, preferred_element_type=jnp.float32)
            * scale_value
        )
        key_sum, value_sum = carry
        key_sum = (
            key_sum
            + jnp.einsum(
                "hqk,qhd->khd", grad_scores, query_block, preferred_element_type=jnp.float32
            )
            * scale_value
        )
        value_sum = value_sum + jnp.einsum(
            "hqk,qhd->khd",
            probs.astype(jnp.bfloat16),
            grad_block,
            preferred_element_type=jnp.float32,
        )
        return ((key_sum, value_sum), grad_query)

    zeros = jnp.zeros(key_heads.shape, jnp.float32)
    (key_sum, value_sum), grad_query = lax.scan(
        one_block, (zeros, zeros), (query_heads, grad_heads, log_norm, jnp.arange(blocks))
    )
    key_total = key_rows.shape[0]
    return (
        grad_query.reshape(row_total, -1),
        key_sum.reshape(key_total, -1),
        value_sum.reshape(key_total, -1),
    )


def widened(shard, dim, factor):
    shape_list = list(shard.shape)
    shape_list[dim] = shape_list[dim] * factor
    return jnp.zeros(shape_list, jnp.float32)


def body(
    inputs,
    memory,
    tgt_len,
    src_len,
    cotangent,
    w_qkv,
    w_out,
    cross_query,
    cross_kv,
    cross_out,
    ffn_up,
    ffn_down,
    gain_one,
    bias_one,
    gain_two,
    bias_two,
    gain_three,
    bias_three,
):
    own_rows = inputs.shape[1]
    row_first = lax.axis_index("tensor") * own_rows
    shards = (
        w_qkv,
        w_out,
        cross_query,
        cross_kv,
        cross_out,
        ffn_up,
        ffn_down,
        gain_one,
        bias_one,
        gain_two,
        bias_two,
        gain_three,
        bias_three,
    )
    shard_dims = (1, 1, 0, 1, 1, 0, 1, 0, 0, 0, 0, 0, 0)
    dp_count = lax.axis_size("dp")
    accum_list = [
        widened(shard, dim_index, dp_count) for shard, dim_index in zip(shards, shard_dims)
    ]
    accum_init = tuple(accum_list)

    def advance(accum, members):
        own_in, own_memory, tgt_count, src_count, own_cot = members
        gathered = gather_weights(*shards)
        live_rows = (row_first + jnp.arange(own_rows) < tgt_count).astype(jnp.float32)[:, None]
        residual_in = own_in.astype(jnp.float32)
        normed, pull_one = jax.vjp(
            layer_norm,
            residual_in,
            gathered[7].astype(jnp.float32),
            gathered[8].astype(jnp.float32),
        )
        normed_all = norm_rows(normed.astype(jnp.bfloat16))
        projected = jnp.einsum(
            "td,jdh->jth", normed_all, gathered[0], preferred_element_type=jnp.float32
        ).astype(jnp.bfloat16)
        self_mix, self_norm = attend_forward(
            projected[0], projected[1], projected[2], True, tgt_count
        )
        hidden_one = residual_in + branch_sum(self_mix, gathered[1])
        normed, pull_two = jax.vjp(
            layer_norm,
            hidden_one,
            gathered[9].astype(jnp.float32),
            gathered[10].astype(jnp.float32),
        )
        cross_all, memory_all = (
            lax.all_gather(normed.astype(jnp.bfloat16), "tensor", axis=0, tiled=True),
            lax.all_gather(own_memory, "tensor", axis=0, tiled=True),
        )
        cross_queries = jnp.dot(cross_all, gathered[2], preferred_element_type=jnp.float32).astype(
            jnp.bfloat16
        )
        cross_pair = jnp.einsum(
            "sd,jdh->jsh", memory_all, gathered[3], preferred_element_type=jnp.float32
        ).astype(jnp.bfloat16)
        cross_mix, cross_norm = attend_forward(
            cross_queries, cross_pair[0], cross_pair[1], False, src_count
        )
        hidden_two = hidden_one + branch_sum(cross_mix, gathered[4])
        normed, pull_three = jax.vjp(
            layer_norm,
            hidden_two,
            gathered[11].astype(jnp.float32),
            gathered[12].astype(jnp.float32),
        )
        grad_out = live_rows * own_cot.astype(jnp.float32)
        ffn_rows = norm_rows(normed.astype(jnp.bfloat16))
        before = jnp.dot(ffn_rows, gathered[5], preferred_element_type=jnp.float32)
        gated, gate_pull = jax.vjp(smooth_gate, before)
        active = gated.astype(jnp.bfloat16)
        output = live_rows * (hidden_two + branch_sum(active, gathered[6]))
        grad_all = grad_rows(grad_out.astype(jnp.bfloat16))
        grad_down = jnp.einsum("tf,td->fd", active, grad_all, preferred_element_type=jnp.float32)
        grad_active = jnp.einsum(
            "td,fd->tf", grad_all, gathered[6], preferred_element_type=jnp.float32
        )
        grad_before = gate_pull(grad_active)[0].astype(jnp.bfloat16)
        grad_up = jnp.einsum("td,tf->df", ffn_rows, grad_before, preferred_element_type=jnp.float32)

        def ffn_term(first_row, row_count):
            return jnp.einsum(
                "tf,df->td", grad_before, gathered[5], preferred_element_type=jnp.float32
            )

        back_three = input_grad(ffn_term, own_rows)
        grad_hidden, grad_gain_three, grad_bias_three = pull_three(back_three)
        grad_two = grad_out + grad_hidden
        grad_all = grad_rows(grad_two.astype(jnp.bfloat16))
        grad_cross = jnp.einsum(
            "th,td->hd", cross_mix, grad_all, preferred_element_type=jnp.float32
        )
        grad_mix = jnp.einsum(
            "td,hd->th", grad_all, gathered[4], preferred_element_type=jnp.float32
        ).astype(jnp.bfloat16)
        grad_cq, grad_ck, grad_cv = attend_backward(
            cross_queries, cross_pair[0], cross_pair[1], grad_mix, cross_norm, False, src_count
        )
        grad_cq = grad_cq.astype(jnp.bfloat16)
        grad_ckv = jnp.stack([grad_ck, grad_cv]).astype(jnp.bfloat16)
        grad_query = jnp.einsum("td,th->dh", cross_all, grad_cq, preferred_element_type=jnp.float32)
        grad_pair = jnp.einsum(
            "sd,jsh->jdh", memory_all, grad_ckv, preferred_element_type=jnp.float32
        )
        back_rows = jnp.einsum(
            "th,dh->td", grad_cq, gathered[2], preferred_element_type=jnp.float32
        )
        back_memory = jnp.einsum(
            "jsh,jdh->sd", grad_ckv, gathered[3], preferred_element_type=jnp.float32
        )
        own_back, grad_encoded = (
            lax.psum_scatter(back_rows, "tensor", scatter_dimension=0, tiled=True),
            lax.psum_scatter(back_memory, "tensor", scatter_dimension=0, tiled=True),
        )
        grad_hidden, grad_gain_two, grad_bias_two = pull_two(own_back)
        grad_one = grad_two + grad_hidden
        grad_all = grad_rows(grad_one.astype(jnp.bfloat16))
        grad_self_out = jnp.einsum(
            "th,td->hd", self_mix, grad_all, preferred_element_type=jnp.float32
        )
        grad_mix = jnp.einsum(
            "td,hd->th", grad_all, gathered[1], preferred_element_type=jnp.float32
        ).astype(jnp.bfloat16)
        grad_sq, grad_sk, grad_sv = attend_backward(
            projected[0], projected[1], projected[2], grad_mix, self_norm, True, tgt_count
        )
        grad_triple = jnp.stack([grad_sq, grad_sk, grad_sv]).astype(jnp.bfloat16)
        grad_qkv = jnp.einsum(
            "td,jth->jdh", normed_all, grad_triple, preferred_element_type=jnp.float32
        )

        def self_term(first_row, row_count):
            return jnp.einsum(
                "jth,jdh->td", grad_triple, gathered[0], preferred_element_type=jnp.float32
            )

        grad_hidden, grad_gain_one, grad_bias_one = pull_one(input_grad(self_term, own_rows))
        grad_values = grad_one + grad_hidden
        grads = (
            grad_qkv,
            grad_self_out,
            grad_query,
            grad_pair,
            grad_cross,
            grad_up,
            grad_down,
            grad_gain_one,
            grad_bias_one,
            grad_gain_two,
            grad_bias_two,
            grad_gain_three,
            grad_bias_three,
        )
        accum = jax.tree.map(jnp.add, accum, grads)
        return (accum, (output.astype(jnp.bfloat16), grad_values, grad_encoded))

    accum, (outputs, grad_inputs, grad_memory) = lax.scan(
        advance, accum_init, (inputs, memory, tgt_len, src_len, cotangent)
    )
    accum_list = list(accum)
    accum = reduce_grads(*accum_list)
    norm_grads = lax.psum((accum[7], accum[8], accum[9], accum[10], accum[11], accum[12]), "tensor")
    return (
        outputs,
        grad_inputs,
        grad_memory,
        accum[0],
        accum[1],
        accum[2],
        accum[3],
        accum[4],
        accum[5],
        accum[6],
        norm_grads[0],
        norm_grads[1],
        norm_grads[2],
        norm_grads[3],
        norm_grads[4],
        norm_grads[5],
    )


def solution(mesh):
    return jax.shard_map(
        body,
        mesh=mesh,
        in_specs=(
            P("dp", "tensor", None),
            P("dp", "tensor", None),
            P("dp"),
            P("dp"),
            P("dp", "tensor", None),
            P(None, "dp", "tensor"),
            P("tensor", "dp"),
            P("dp", "tensor"),
            P(None, "dp", "tensor"),
            P("tensor", "dp"),
            P("dp", "tensor"),
            P("tensor", "dp"),
            P("dp"),
            P("dp"),
            P("dp"),
            P("dp"),
            P("dp"),
            P("dp"),
        ),
        out_specs=(
            P("dp", "tensor", None),
            P("dp", "tensor", None),
            P("dp", "tensor", None),
            P(None, "dp", "tensor"),
            P("tensor", "dp"),
            P("dp", "tensor"),
            P(None, "dp", "tensor"),
            P("tensor", "dp"),
            P("dp", "tensor"),
            P("tensor", "dp"),
            P("dp"),
            P("dp"),
            P("dp"),
            P("dp"),
            P("dp"),
            P("dp"),
        ),
        check_vma=False,
    )
```

profile of v0, /device:TPU:0, one launch (start us, length us, event | category | flops | bytes accessed | tf_op | source)
XLA Modules:
  0.0 1706.3 jit_solution(2830867907719155688)
XLA Ops:
  8.2 1231.4 %while.159 = (s32[]{:T(128)}, f32[3,512,128]{1,2,0:T(8,128)}, f32[128,512]{1,0:T(8,128)}, f32[512,128]{1,0:T(8,128)}, f32[2,512,128]{1,2,0:T(8,128)}, /*index=5*...) while((s32[]{:T(128)}, f32[3,512,128]{1,2,0:T(8,128)}, ...), condition=%wide.region_40.41_spmd.clone, body=%wide.region_0.40_spmd.clone.sunk | while | flops 8421522944 | bytes 381262368 | solution.py:389
  41.5 23.9 %all-reduce.22 = (bf16[512]{0:T(512)(128)(2,1)S(1)}, bf16[512]{0:T(512)(128)(2,1)S(1)}, bf16[512]{0:T(512)(128)(2,1)S(1)}, bf16[512]{0:T(512)(128)(2,1)S(1)}, bf...) all-reduce(bf16[512]{0:T(512)(128)(2,1)S(1)} %dynamic-update-slice.18, ...), channel_id=1, replica_groups=mesh['dp'=8,'tensor'=4] {'dp'}, use_global_device_ids=true, to_apply=%add.1 | all-reduce | flops 3072 | bytes 12288 | tf_op jit(solution)/shard_map/while
  68.6 30.7 %all_gather.148 = bf16[128,512]{0,1:T(8,128)(2,1)S(1)} all-gather(bf16[128,64]{0,1:T(8,128)(2,1)} %get-tuple-element.2082), channel_id=1, replica_groups=mesh['dp'=8,'tensor'=4] {'dp'}, dimensions={1}, use_global_device_ids=true | all-gather | bytes 147456 | tf_op jit(solution)/shard_map/while/body/eval_jaxpr/all_gather | solution.py:41
  99.3 31.2 %all_gather.147 = bf16[3,512,128]{2,1,0:T(8,128)(2,1)S(1)} all-gather(bf16[3,64,128]{2,1,0:T(8,128)(2,1)} %get-tuple-element.2077), channel_id=1, replica_groups=mesh['dp'=8,'tensor'=4] {'dp'}, dimensions={1}, use_global_device_ids=true | all-gather | bytes 442368 | tf_op jit(solution)/shard_map/while/body/eval_jaxpr/all_gather | solution.py:40
  133.4 12.2 while.160
  149.5 27.9 %reduce-scatter.29.cloned.1.call-done = f32[256,512]{1,0:T(8,128)} async-done(((f32[1024,512]{1,0:T(8,128)}), f32[256,512]{1,0:T(8,128)}) %reduce-scatter.29.cloned.1.call-update) | async-done | bytes 524304 | tf_op jit(solution)/shard_map/while/body/eval_jaxpr/reduce_scatter | solution.py:97
  180.4 30.6 %all_gather.154 = bf16[128,512]{0,1:T(8,128)(2,1)S(1)} all-gather(bf16[128,64]{0,1:T(8,128)(2,1)S(1)} %copy-done.65), channel_id=1, replica_groups=mesh['dp'=8,'tensor'=4] {'dp'}, dimensions={1}, use_global_device_ids=true | all-gather | bytes 147456 | tf_op jit(solution)/shard_map/while/body/eval_jaxpr/all_gather | solution.py:44
  210.9 30.5 %all_gather.150 = bf16[512,128]{1,0:T(8,128)(2,1)S(1)} all-gather(bf16[64,128]{1,0:T(8,128)(2,1)S(1)} %copy-done.64), channel_id=1, replica_groups=mesh['dp'=8,'tensor'=4] {'dp'}, dimensions={0}, use_global_device_ids=true | all-gather | bytes 147456 | tf_op jit(solution)/shard_map/while/body/eval_jaxpr/all_gather | solution.py:42
  241.4 30.7 %all_gather.151 = bf16[2,512,128]{2,1,0:T(8,128)(2,1)S(1)} all-gather(bf16[2,64,128]{2,1,0:T(8,128)(2,1)S(1)} %copy-done.50), channel_id=1, replica_groups=mesh['dp'=8,'tensor'=4] {'dp'}, dimensions={1}, use_global_device_ids=true | all-gather | bytes 294912 | tf_op jit(solution)/shard_map/while/body/eval_jaxpr/all_gather | solution.py:43
  276.5 8.1 while.161
  290.4 28.5 %reduce-scatter.31.cloned.1.call-done = f32[256,512]{1,0:T(8,128)} async-done(((f32[1024,512]{1,0:T(8,128)}), f32[256,512]{1,0:T(8,128)}) %reduce-scatter.31.cloned.1.call-update) | async-done | bytes 524304 | tf_op jit(solution)/shard_map/while/body/eval_jaxpr/reduce_scatter | solution.py:97
  321.3 33.6 %all_gather.156 = bf16[512,512]{1,0:T(8,128)(2,1)} all-gather(bf16[64,512]{1,0:T(8,128)(2,1)S(1)} %copy-done.38), channel_id=1, replica_groups=mesh['dp'=8,'tensor'=4] {'dp'}, dimensions={0}, use_global_device_ids=true | all-gather | bytes 589824 | tf_op jit(solution)/shard_map/while/body/eval_jaxpr/all_gather | solution.py:45
  355.0 31.2 %all_gather.153 = bf16[512,512]{0,1:T(8,128)(2,1)S(1)} all-gather(bf16[512,64]{0,1:T(8,128)(2,1)S(1)} %copy-done.37), channel_id=1, replica_groups=mesh['dp'=8,'tensor'=4] {'dp'}, dimensions={1}, use_global_device_ids=true | all-gather | bytes 589824 | tf_op jit(solution)/shard_map/while/body/eval_jaxpr/all_gather | solution.py:46
  386.2 3.5 fusion.336
  389.7 5.3 fusion.340
  398.1 31.7 %reduce-scatter.33.cloned.1.call-done = f32[256,512]{1,0:T(8,128)} async-done(((f32[1024,512]{1,0:T(8,128)}), f32[256,512]{1,0:T(8,128)}) %reduce-scatter.33.cloned.1.call-update) | async-done | bytes 524304 | tf_op jit(solution)/shard_map/while/body/eval_jaxpr/reduce_scatter | solution.py:106
  434.7 16.8 all-gather.22.cloned.1.call-done
  457.9 13.5 while.162
  472.8 2.8 fusion.344
  475.6 31.5 %reduce-scatter.35.cloned.1.call-done = f32[256,512]{1,0:T(8,128)} async-done(((f32[1024,512]{1,0:T(8,128)}), f32[256,512]{1,0:T(8,128)}) %reduce-scatter.35.cloned.1.call-update) | async-done | bytes 524304 | tf_op jit(solution)/shard_map/while/body/eval_jaxpr/reduce_scatter | solution.py:344
  512.5 3.9 fusion.351
  520.3 9.0 all-gather.24.cloned.1.call-done
  532.4 21.7 %while.163 = (s32[]{:T(128)}, f32[1024,2,64]{0,2,1:T(8,128)S(1)}, f32[1024,2,64]{0,2,1:T(8,128)}, bf16[2,512,2,64]{1,3,2,0:T(8,128)(2,1)}, bf16[2,512,2,64]{1,3,...) while((s32[]{:T(128)}, f32[1024,2,64]{0,2,1:T(8,128)S(1)}, ...), condition=%wide.region_28.28_spmd.clone, body=%wide.region_26.27_spmd.clone.sunk | while | flops 688587264 | bytes 37259468 | solution.py:193
  545.8 3.2 fusion.389
  559.8 3.1 convolution_add_fusion.13
  573.1 24.2 %reduce-scatter.41.cloned.1.call-done = f32[256,512]{1,0:T(8,128)} async-done(((f32[1024,512]{1,0:T(8,128)}), f32[256,512]{1,0:T(8,128)}) %reduce-scatter.41.cloned.1.call-update) | async-done | bytes 524304 | tf_op jit(solution)/shard_map/while/body/eval_jaxpr/reduce_scatter | solution.py:345
  601.6 2.9 fusion.347
  604.5 26.7 %reduce-scatter.37.cloned.1.call-done = f32[256,512]{1,0:T(8,128)} async-done(((f32[1024,512]{1,0:T(8,128)}), f32[256,512]{1,0:T(8,128)}) %reduce-scatter.37.cloned.1.call-update) | async-done | bytes 524304 | tf_op jit(solution)/shard_map/while/body/eval_jaxpr/reduce_scatter | solution.py:106
  645.6 22.1 %all-reduce.22 = (bf16[512]{0:T(512)(128)(2,1)S(1)}, bf16[512]{0:T(512)(128)(2,1)S(1)}, bf16[512]{0:T(512)(128)(2,1)S(1)}, bf16[512]{0:T(512)(128)(2,1)S(1)}, bf...) all-reduce(bf16[512]{0:T(512)(128)(2,1)S(1)} %dynamic-update-slice.18, ...), channel_id=1, replica_groups=mesh['dp'=8,'tensor'=4] {'dp'}, use_global_device_ids=true, to_apply=%add.1 | all-reduce | flops 3072 | bytes 12288 | tf_op jit(solution)/shard_map/while
  670.9 30.7 %all_gather.148 = bf16[128,512]{0,1:T(8,128)(2,1)S(1)} all-gather(bf16[128,64]{0,1:T(8,128)(2,1)} %get-tuple-element.2082), channel_id=1, replica_groups=mesh['dp'=8,'tensor'=4] {'dp'}, dimensions={1}, use_global_device_ids=true | all-gather | bytes 147456 | tf_op jit(solution)/shard_map/while/body/eval_jaxpr/all_gather | solution.py:41
  701.6 31.2 %all_gather.147 = bf16[3,512,128]{2,1,0:T(8,128)(2,1)S(1)} all-gather(bf16[3,64,128]{2,1,0:T(8,128)(2,1)} %get-tuple-element.2077), channel_id=1, replica_groups=mesh['dp'=8,'tensor'=4] {'dp'}, dimensions={1}, use_global_device_ids=true | all-gather | bytes 442368 | tf_op jit(solution)/shard_map/while/body/eval_jaxpr/all_gather | solution.py:40
  735.7 12.2 while.160
  751.7 27.0 %reduce-scatter.29.cloned.1.call-done = f32[256,512]{1,0:T(8,128)} async-done(((f32[1024,512]{1,0:T(8,128)}), f32[256,512]{1,0:T(8,128)}) %reduce-scatter.29.cloned.1.call-update) | async-done | bytes 524304 | tf_op jit(solution)/shard_map/while/body/eval_jaxpr/reduce_scatter | solution.py:97
  781.7 30.6 %all_gather.154 = bf16[128,512]{0,1:T(8,128)(2,1)S(1)} all-gather(bf16[128,64]{0,1:T(8,128)(2,1)S(1)} %copy-done.65), channel_id=1, replica_groups=mesh['dp'=8,'tensor'=4] {'dp'}, dimensions={1}, use_global_device_ids=true | all-gather | bytes 147456 | tf_op jit(solution)/shard_map/while/body/eval_jaxpr/all_gather | solution.py:44
  812.3 30.5 %all_gather.150 = bf16[512,128]{1,0:T(8,128)(2,1)S(1)} all-gather(bf16[64,128]{1,0:T(8,128)(2,1)S(1)} %copy-done.64), channel_id=1, replica_groups=mesh['dp'=8,'tensor'=4] {'dp'}, dimensions={0}, use_global_device_ids=true | all-gather | bytes 147456 | tf_op jit(solution)/shard_map/while/body/eval_jaxpr/all_gather | solution.py:42
  842.8 30.7 %all_gather.151 = bf16[2,512,128]{2,1,0:T(8,128)(2,1)S(1)} all-gather(bf16[2,64,128]{2,1,0:T(8,128)(2,1)S(1)} %copy-done.50), channel_id=1, replica_groups=mesh['dp'=8,'tensor'=4] {'dp'}, dimensions={1}, use_global_device_ids=true | all-gather | bytes 294912 | tf_op jit(solution)/shard_map/while/body/eval_jaxpr/all_gather | solution.py:43
  877.8 8.1 while.161
  891.8 28.5 %reduce-scatter.31.cloned.1.call-done = f32[256,512]{1,0:T(8,128)} async-done(((f32[1024,512]{1,0:T(8,128)}), f32[256,512]{1,0:T(8,128)}) %reduce-scatter.31.cloned.1.call-update) | async-done | bytes 524304 | tf_op jit(solution)/shard_map/while/body/eval_jaxpr/reduce_scatter | solution.py:97
  922.7 33.6 %all_gather.156 = bf16[512,512]{1,0:T(8,128)(2,1)} all-gather(bf16[64,512]{1,0:T(8,128)(2,1)S(1)} %copy-done.38), channel_id=1, replica_groups=mesh['dp'=8,'tensor'=4] {'dp'}, dimensions={0}, use_global_device_ids=true | all-gather | bytes 589824 | tf_op jit(solution)/shard_map/while/body/eval_jaxpr/all_gather | solution.py:45
  956.3 31.2 %all_gather.153 = bf16[512,512]{0,1:T(8,128)(2,1)S(1)} all-gather(bf16[512,64]{0,1:T(8,128)(2,1)S(1)} %copy-done.37), channel_id=1, replica_groups=mesh['dp'=8,'tensor'=4] {'dp'}, dimensions={1}, use_global_device_ids=true | all-gather | bytes 589824 | tf_op jit(solution)/shard_map/while/body/eval_jaxpr/all_gather | solution.py:46
  987.5 3.5 fusion.336
  991.0 5.3 fusion.340
  999.4 31.6 %reduce-scatter.33.cloned.1.call-done = f32[256,512]{1,0:T(8,128)} async-done(((f32[1024,512]{1,0:T(8,128)}), f32[256,512]{1,0:T(8,128)}) %reduce-scatter.33.cloned.1.call-update) | async-done | bytes 524304 | tf_op jit(solution)/shard_map/while/body/eval_jaxpr/reduce_scatter | solution.py:106
  1036.0 16.8 all-gather.22.cloned.1.call-done
  1059.2 13.5 while.162
  1074.0 2.8 fusion.344
  1076.9 31.5 %reduce-scatter.35.cloned.1.call-done = f32[256,512]{1,0:T(8,128)} async-done(((f32[1024,512]{1,0:T(8,128)}), f32[256,512]{1,0:T(8,128)}) %reduce-scatter.35.cloned.1.call-update) | async-done | bytes 524304 | tf_op jit(solution)/shard_map/while/body/eval_jaxpr/reduce_scatter | solution.py:344
  1113.8 3.9 fusion.351
  1121.6 9.0 all-gather.24.cloned.1.call-done
  1133.7 21.7 %while.163 = (s32[]{:T(128)}, f32[1024,2,64]{0,2,1:T(8,128)S(1)}, f32[1024,2,64]{0,2,1:T(8,128)}, bf16[2,512,2,64]{1,3,2,0:T(8,128)(2,1)}, bf16[2,512,2,64]{1,3,...) while((s32[]{:T(128)}, f32[1024,2,64]{0,2,1:T(8,128)S(1)}, ...), condition=%wide.region_28.28_spmd.clone, body=%wide.region_26.27_spmd.clone.sunk | while | flops 688587264 | bytes 37259468 | solution.py:193
  1147.1 3.2 fusion.389
  1161.1 3.5 convolution_add_fusion.13
  1175.7 22.8 %reduce-scatter.41.cloned.1.call-done = f32[256,512]{1,0:T(8,128)} async-done(((f32[1024,512]{1,0:T(8,128)}), f32[256,512]{1,0:T(8,128)}) %reduce-scatter.41.cloned.1.call-update) | async-done | bytes 524304 | tf_op jit(solution)/shard_map/while/body/eval_jaxpr/reduce_scatter | solution.py:345
  1202.8 3.1 fusion.347
  1205.9 26.6 %reduce-scatter.37.cloned.1.call-done = f32[256,512]{1,0:T(8,128)} async-done(((f32[1024,512]{1,0:T(8,128)}), f32[256,512]{1,0:T(8,128)}) %reduce-scatter.37.cloned.1.call-update) | async-done | bytes 524304 | tf_op jit(solution)/shard_map/while/body/eval_jaxpr/reduce_scatter | solution.py:106
  1251.9 37.1 %all-reduce.19 = (f32[512]{0:T(512)S(1)}, f32[512]{0:T(512)S(1)}, f32[512]{0:T(512)S(1)}, f32[512]{0:T(512)S(1)}, f32[512]{0:T(512)S(1)}, /*index=5*/f32[512]{0:T(512)S(1)}) all-reduce(f32[512]{0:T(512)S(1)} %copy-done.95, f32[512]{0:T(512)S(1)} %copy-done.92, ...), channel_id=17, replica_groups=mesh['dp'=8,'tensor'=4] {'dp'}, use_global_device_ids=true, to_apply=%region_48.49.clone | all-reduce | flops 3072 | bytes 24576
  1289.4 6.4 all-reduce.20
  1295.9 9.5 reduce-scatter.19.cloned.1.call-done
  1305.4 64.1 %reduce-scatter.17.cloned.1.call-done = f32[128,64]{0,1:T(8,128)} async-done(((f32[128,512]{0,1:T(8,128)}), f32[128,64]{0,1:T(8,128)}) %reduce-scatter.17.cloned.1.call-update) | async-done | bytes 32784 | tf_op jit(solution)/shard_map/reduce_scatter | solution.py:73
  1369.5 64.2 %reduce-scatter.23.cloned.1.call-done = f32[128,64]{0,1:T(8,128)} async-done(((f32[128,512]{0,1:T(8,128)}), f32[128,64]{0,1:T(8,128)}) %reduce-scatter.23.cloned.1.call-update) | async-done | bytes 32784 | tf_op jit(solution)/shard_map/reduce_scatter | solution.py:76
  1433.7 65.0 %reduce-scatter.21.cloned.1.call-done = f32[2,64,128]{2,1,0:T(8,128)} async-done(((f32[2,512,128]{2,1,0:T(8,128)}), f32[2,64,128]{2,1,0:T(8,128)}) %reduce-scatter.21.cloned.1.call-update) | async-done | bytes 65552 | tf_op jit(solution)/shard_map/reduce_scatter | solution.py:75
  1498.7 66.6 %reduce-scatter.15.cloned.1.call-done = f32[3,64,128]{2,1,0:T(8,128)} async-done(((f32[3,512,128]{2,1,0:T(8,128)}), f32[3,64,128]{2,1,0:T(8,128)}) %reduce-scatter.15.cloned.1.call-update) | async-done | bytes 98320 | tf_op jit(solution)/shard_map/reduce_scatter | solution.py:72
  1565.3 66.6 %reduce-scatter.25.cloned.1.call-done = f32[64,512]{1,0:T(8,128)} async-done(((f32[512,512]{1,0:T(8,128)}), f32[64,512]{1,0:T(8,128)}) %reduce-scatter.25.cloned.1.call-update) | async-done | bytes 131088 | tf_op jit(solution)/shard_map/reduce_scatter | solution.py:77
  1631.9 66.8 %reduce-scatter.27.cloned.1.call-done = f32[512,64]{0,1:T(8,128)} async-done(((f32[512,512]{0,1:T(8,128)}), f32[512,64]{0,1:T(8,128)}) %reduce-scatter.27.cloned.1.call-update) | async-done | bytes 131088 | tf_op jit(solution)/shard_map/reduce_scatter | solution.py:78
  (856 shorter events, 283.5 us)
Async XLA Ops:
  32.2 98.4 %all-gather.12.cloned.1.call-start = ((), (), s32[]{:S(2)}) async-start(), calls=%async_computation.21 | async-start | bytes 1310720 | tf_op jit(solution)/shard_map/while/body/eval_jaxpr/all_gather | solution.py:89
  33.3 66.0 %copy-start.44 = (f32[256]{0:T(256)}, f32[256]{0:T(256)S(1)}, u32[]{:S(2)}) copy-start(f32[256]{0:T(256)S(1)} %broadcast_multiply_fusion.6) | copy-start | bytes 3076 | tf_op jit(solution)/shard_map/while
  34.5 64.8 %copy-start.58 = (f32[256]{0:T(256)}, f32[256]{0:T(256)S(1)}, u32[]{:S(2)}) copy-start(f32[256]{0:T(256)S(1)} %fusion.326) | copy-start | bytes 3076 | tf_op jit(solution)/shard_map/while
  67.3 110.1 %reduce-scatter.29.cloned.1.call-start = ((), (), s32[]{:S(2)}) async-start(), calls=%async_computation.22 | async-start | bytes 2621440 | tf_op jit(solution)/shard_map/while/body/eval_jaxpr/reduce_scatter | solution.py:97
  146.8 64.2 %copy-start.64 = (bf16[64,128]{1,0:T(8,128)(2,1)S(1)}, bf16[64,128]{1,0:T(8,128)(2,1)}, u32[]{:S(2)}) copy-start(bf16[64,128]{1,0:T(8,128)(2,1)} %get-tuple-element.2085) | copy-start | bytes 49156 | tf_op jit(solution)/shard_map/while
  146.8 94.7 %copy-start.50 = (bf16[2,64,128]{2,1,0:T(8,128)(2,1)S(1)}, bf16[2,64,128]{2,1,0:T(8,128)(2,1)}, u32[]{:S(2)}) copy-start(bf16[2,64,128]{2,1,0:T(8,128)(2,1)} %get-tuple-element.2087) | copy-start | bytes 98308 | tf_op jit(solution)/shard_map/while
  148.6 123.6 %all-gather.16.cloned.1.call-start = ((), (), s32[]{:S(2)}) async-start(), calls=%async_computation.24 | async-start | bytes 1310720 | tf_op jit(solution)/shard_map/while/body/eval_jaxpr/all_gather | solution.py:281
  149.4 124.7 %all-gather.14.cloned.1.call-start = ((), (), s32[]{:S(2)}) async-start(), calls=%async_computation.23 | async-start | bytes 1310720 | tf_op jit(solution)/shard_map/while/body/eval_jaxpr/all_gather | solution.py:280
  149.5 126.5 %copy-start.46 = (f32[512]{0:T(512)}, f32[512]{0:T(512)S(1)}, u32[]{:S(2)}) copy-start(f32[512]{0:T(512)S(1)} %convert_element_type.395) | copy-start | bytes 6148 | tf_op jit(solution)/shard_map/while
  178.6 97.8 %copy-start.54 = (f32[256]{0:T(256)}, f32[256]{0:T(256)S(1)}, u32[]{:S(2)}) copy-start(f32[256]{0:T(256)S(1)} %broadcast_multiply_fusion.7) | copy-start | bytes 3076 | tf_op jit(solution)/shard_map/while
  178.8 97.6 %copy-start.70 = (f32[256]{0:T(256)}, f32[256]{0:T(256)S(1)}, u32[]{:S(2)}) copy-start(f32[256]{0:T(256)S(1)} %multiply_reduce_fusion.14) | copy-start | bytes 3076 | tf_op jit(solution)/shard_map/while
  178.8 97.6 %copy-start.60 = (f32[256]{0:T(256)}, f32[256]{0:T(256)S(1)}, u32[]{:S(2)}) copy-start(f32[256]{0:T(256)S(1)} %fusion.332) | copy-start | bytes 3076 | tf_op jit(solution)/shard_map/while
  179.7 139.2 %reduce-scatter.31.cloned.1.call-start = ((), (), s32[]{:S(2)}) async-start(), calls=%async_computation.26 | async-start | bytes 2621440 | tf_op jit(solution)/shard_map/while/body/eval_jaxpr/reduce_scatter | solution.py:97
  285.6 69.4 %copy-start.37 = (bf16[512,64]{0,1:T(8,128)(2,1)S(1)}, bf16[512,64]{0,1:T(8,128)(2,1)}, u32[]{:S(2)}) copy-start(bf16[512,64]{0,1:T(8,128)(2,1)} %get-tuple-element.2081) | copy-start | bytes 196612 | tf_op jit(solution)/shard_map/while
  287.4 98.8 %all-gather.18.cloned.1.call-start = ((), (), s32[]{:S(2)}) async-start(), calls=%async_computation.25 | async-start | bytes 1310720 | tf_op jit(solution)/shard_map/while/body/eval_jaxpr/all_gather | solution.py:93
  289.0 100.7 %all-gather.20.cloned.1.call-start = ((), (), s32[]{:S(2)}) async-start(), calls=%async_computation.27 | async-start | bytes 1310720 | tf_op jit(solution)/shard_map/while/body/eval_jaxpr/all_gather | solution.py:89
  289.7 65.2 %copy-start.48 = (f32[512]{0:T(512)}, f32[512]{0:T(512)S(1)}, u32[]{:S(2)}) copy-start(f32[512]{0:T(512)S(1)} %convert_element_type.397) | copy-start | bytes 6148 | tf_op jit(solution)/shard_map/while
  321.3 108.5 %reduce-scatter.33.cloned.1.call-start = ((), (), s32[]{:S(2)}) async-start(), calls=%async_computation.28 | async-start | bytes 2621440 | tf_op jit(solution)/shard_map/while/body/eval_jaxpr/reduce_scatter | solution.py:106
  398.0 53.5 %all-gather.22.cloned.1.call-start = ((), (), s32[]{:S(2)}) async-start(), calls=%async_computation.29 | async-start | bytes 1310720 | tf_op jit(solution)/shard_map/while/body/eval_jaxpr/all_gather | solution.py:93
  434.6 72.5 %reduce-scatter.35.cloned.1.call-start = ((), (), s32[]{:S(2)}) async-start(), calls=%async_computation.30 | async-start | bytes 2621440 | tf_op jit(solution)/shard_map/while/body/eval_jaxpr/reduce_scatter | solution.py:344
  475.6 53.8 %all-gather.24.cloned.1.call-start = ((), (), s32[]{:S(2)}) async-start(), calls=%async_computation.31 | async-start | bytes 1310720 | tf_op jit(solution)/shard_map/while/body/eval_jaxpr/all_gather | solution.py:93
  512.4 52.8 %reduce-scatter.39.cloned.1.call-start = ((), (), s32[]{:S(2)}) async-start(), calls=%async_computation.33 | async-start | bytes 2621440 | tf_op jit(solution)/shard_map/while/body/eval_jaxpr/reduce_scatter | solution.py:97
  516.4 80.9 %reduce-scatter.41.cloned.1.call-start = ((), (), s32[]{:S(2)}) async-start(), calls=%async_computation.34 | async-start | bytes 2621440 | tf_op jit(solution)/shard_map/while/body/eval_jaxpr/reduce_scatter | solution.py:345
  520.3 110.9 %reduce-scatter.37.cloned.1.call-start = ((), (), s32[]{:S(2)}) async-start(), calls=%async_computation.32 | async-start | bytes 2621440 | tf_op jit(solution)/shard_map/while/body/eval_jaxpr/reduce_scatter | solution.py:106
  573.0 58.2 %copy-start.1 = (bf16[2,256,512]{2,1,0:T(8,128)(2,1)S(1)}, bf16[2,256,512]{2,1,0:T(8,128)(2,1)}, u32[]{:S(2)}) copy-start(bf16[2,256,512]{2,1,0:T(8,128)(2,1)} %get-tuple-element.2074) | copy-start | bytes 1572868 | tf_op jit(solution)/shard_map/while
  573.0 58.2 %copy-start.40 = (f32[512]{0:T(512)S(1)}, f32[512]{0:T(512)}, u32[]{:S(2)}) copy-start(f32[512]{0:T(512)} %copy-done.39) | copy-start | bytes 6148 | tf_op jit(solution)/shard_map/while
  573.0 58.2 %copy-start.45 = (f32[256]{0:T(256)S(1)}, f32[256]{0:T(256)}, u32[]{:S(2)}) copy-start(f32[256]{0:T(256)} %copy-done.44) | copy-start | bytes 3076 | tf_op jit(solution)/shard_map/while
  573.0 59.5 %copy-start.69 = (f32[256]{0:T(256)S(1)}, f32[256]{0:T(256)}, u32[]{:S(2)}) copy-start(f32[256]{0:T(256)} %copy-done.68) | copy-start | bytes 3076 | tf_op jit(solution)/shard_map/while
  573.0 59.5 %copy-start.59 = (f32[256]{0:T(256)S(1)}, f32[256]{0:T(256)}, u32[]{:S(2)}) copy-start(f32[256]{0:T(256)} %copy-done.58) | copy-start | bytes 3076 | tf_op jit(solution)/shard_map/while
  573.1 60.8 %copy-start.85 = (f32[512]{0:T(512)}, f32[512]{0:T(512)S(1)}, u32[]{:S(2)}) copy-start(f32[512]{0:T(512)S(1)} %get-tuple-element.2068) | copy-start | bytes 6148 | tf_op jit(solution)/shard_map/while
  573.1 60.8 %copy-start.88 = (f32[512]{0:T(512)}, f32[512]{0:T(512)S(1)}, u32[]{:S(2)}) copy-start(f32[512]{0:T(512)S(1)} %get-tuple-element.2067) | copy-start | bytes 6148 | tf_op jit(solution)/shard_map/while
  636.2 96.5 %all-gather.12.cloned.1.call-start = ((), (), s32[]{:S(2)}) async-start(), calls=%async_computation.21 | async-start | bytes 1310720 | tf_op jit(solution)/shard_map/while/body/eval_jaxpr/all_gather | solution.py:89
  637.3 64.3 %copy-start.44 = (f32[256]{0:T(256)}, f32[256]{0:T(256)S(1)}, u32[]{:S(2)}) copy-start(f32[256]{0:T(256)S(1)} %broadcast_multiply_fusion.6) | copy-start | bytes 3076 | tf_op jit(solution)/shard_map/while
  638.5 63.1 %copy-start.58 = (f32[256]{0:T(256)}, f32[256]{0:T(256)S(1)}, u32[]{:S(2)}) copy-start(f32[256]{0:T(256)S(1)} %fusion.326) | copy-start | bytes 3076 | tf_op jit(solution)/shard_map/while
  669.6 109.1 %reduce-scatter.29.cloned.1.call-start = ((), (), s32[]{:S(2)}) async-start(), calls=%async_computation.22 | async-start | bytes 2621440 | tf_op jit(solution)/shard_map/while/body/eval_jaxpr/reduce_scatter | solution.py:97
  749.0 63.3 %copy-start.64 = (bf16[64,128]{1,0:T(8,128)(2,1)S(1)}, bf16[64,128]{1,0:T(8,128)(2,1)}, u32[]{:S(2)}) copy-start(bf16[64,128]{1,0:T(8,128)(2,1)} %get-tuple-element.2085) | copy-start | bytes 49156 | tf_op jit(solution)/shard_map/while
  749.0 93.8 %copy-start.50 = (bf16[2,64,128]{2,1,0:T(8,128)(2,1)S(1)}, bf16[2,64,128]{2,1,0:T(8,128)(2,1)}, u32[]{:S(2)}) copy-start(bf16[2,64,128]{2,1,0:T(8,128)(2,1)} %get-tuple-element.2087) | copy-start | bytes 98308 | tf_op jit(solution)/shard_map/while
  750.8 122.7 %all-gather.16.cloned.1.call-start = ((), (), s32[]{:S(2)}) async-start(), calls=%async_computation.24 | async-start | bytes 1310720 | tf_op jit(solution)/shard_map/while/body/eval_jaxpr/all_gather | solution.py:281
  751.7 123.8 %all-gather.14.cloned.1.call-start = ((), (), s32[]{:S(2)}) async-start(), calls=%async_computation.23 | async-start | bytes 1310720 | tf_op jit(solution)/shard_map/while/body/eval_jaxpr/all_gather | solution.py:280
  751.7 125.6 %copy-start.46 = (f32[512]{0:T(512)}, f32[512]{0:T(512)S(1)}, u32[]{:S(2)}) copy-start(f32[512]{0:T(512)S(1)} %convert_element_type.395) | copy-start | bytes 6148 | tf_op jit(solution)/shard_map/while
  779.9 97.8 %copy-start.54 = (f32[256]{0:T(256)}, f32[256]{0:T(256)S(1)}, u32[]{:S(2)}) copy-start(f32[256]{0:T(256)S(1)} %broadcast_multiply_fusion.7) | copy-start | bytes 3076 | tf_op jit(solution)/shard_map/while
  780.1 97.7 %copy-start.70 = (f32[256]{0:T(256)}, f32[256]{0:T(256)S(1)}, u32[]{:S(2)}) copy-start(f32[256]{0:T(256)S(1)} %multiply_reduce_fusion.14) | copy-start | bytes 3076 | tf_op jit(solution)/shard_map/while
  780.1 97.6 %copy-start.60 = (f32[256]{0:T(256)}, f32[256]{0:T(256)S(1)}, u32[]{:S(2)}) copy-start(f32[256]{0:T(256)S(1)} %fusion.332) | copy-start | bytes 3076 | tf_op jit(solution)/shard_map/while
  781.0 139.2 %reduce-scatter.31.cloned.1.call-start = ((), (), s32[]{:S(2)}) async-start(), calls=%async_computation.26 | async-start | bytes 2621440 | tf_op jit(solution)/shard_map/while/body/eval_jaxpr/reduce_scatter | solution.py:97
  886.9 69.4 %copy-start.37 = (bf16[512,64]{0,1:T(8,128)(2,1)S(1)}, bf16[512,64]{0,1:T(8,128)(2,1)}, u32[]{:S(2)}) copy-start(bf16[512,64]{0,1:T(8,128)(2,1)} %get-tuple-element.2081) | copy-start | bytes 196612 | tf_op jit(solution)/shard_map/while
  888.8 98.8 %all-gather.18.cloned.1.call-start = ((), (), s32[]{:S(2)}) async-start(), calls=%async_computation.25 | async-start | bytes 1310720 | tf_op jit(solution)/shard_map/while/body/eval_jaxpr/all_gather | solution.py:93
  890.3 100.7 %all-gather.20.cloned.1.call-start = ((), (), s32[]{:S(2)}) async-start(), calls=%async_computation.27 | async-start | bytes 1310720 | tf_op jit(solution)/shard_map/while/body/eval_jaxpr/all_gather | solution.py:89
  891.1 65.2 %copy-start.48 = (f32[512]{0:T(512)}, f32[512]{0:T(512)S(1)}, u32[]{:S(2)}) copy-start(f32[512]{0:T(512)S(1)} %convert_element_type.397) | copy-start | bytes 6148 | tf_op jit(solution)/shard_map/while
  922.6 108.5 %reduce-scatter.33.cloned.1.call-start = ((), (), s32[]{:S(2)}) async-start(), calls=%async_computation.28 | async-start | bytes 2621440 | tf_op jit(solution)/shard_map/while/body/eval_jaxpr/reduce_scatter | solution.py:106
  999.4 53.4 %all-gather.22.cloned.1.call-start = ((), (), s32[]{:S(2)}) async-start(), calls=%async_computation.29 | async-start | bytes 1310720 | tf_op jit(solution)/shard_map/while/body/eval_jaxpr/all_gather | solution.py:93
  1035.9 72.5 %reduce-scatter.35.cloned.1.call-start = ((), (), s32[]{:S(2)}) async-start(), calls=%async_computation.30 | async-start | bytes 2621440 | tf_op jit(solution)/shard_map/while/body/eval_jaxpr/reduce_scatter | solution.py:344
  1076.8 53.8 %all-gather.24.cloned.1.call-start = ((), (), s32[]{:S(2)}) async-start(), calls=%async_computation.31 | async-start | bytes 1310720 | tf_op jit(solution)/shard_map/while/body/eval_jaxpr/all_gather | solution.py:93
  1113.7 53.1 %reduce-scatter.39.cloned.1.call-start = ((), (), s32[]{:S(2)}) async-start(), calls=%async_computation.33 | async-start | bytes 2621440 | tf_op jit(solution)/shard_map/while/body/eval_jaxpr/reduce_scatter | solution.py:97
  1117.7 80.8 %reduce-scatter.41.cloned.1.call-start = ((), (), s32[]{:S(2)}) async-start(), calls=%async_computation.34 | async-start | bytes 2621440 | tf_op jit(solution)/shard_map/while/body/eval_jaxpr/reduce_scatter | solution.py:345
  1121.6 110.9 %reduce-scatter.37.cloned.1.call-start = ((), (), s32[]{:S(2)}) async-start(), calls=%async_computation.32 | async-start | bytes 2621440 | tf_op jit(solution)/shard_map/while/body/eval_jaxpr/reduce_scatter | solution.py:106
  1175.7 59.5 %copy-start.85 = (f32[512]{0:T(512)}, f32[512]{0:T(512)S(1)}, u32[]{:S(2)}) copy-start(f32[512]{0:T(512)S(1)} %get-tuple-element.2068) | copy-start | bytes 6148 | tf_op jit(solution)/shard_map/while
  1175.7 59.5 %copy-start.88 = (f32[512]{0:T(512)}, f32[512]{0:T(512)S(1)}, u32[]{:S(2)}) copy-start(f32[512]{0:T(512)S(1)} %get-tuple-element.2067) | copy-start | bytes 6148 | tf_op jit(solution)/shard_map/while
  1239.6 65.8 %reduce-scatter.19.cloned.1.call-start = ((), (), s32[]{:S(2)}) async-start(), calls=%async_computation.16 | async-start | bytes 294912 | tf_op jit(solution)/shard_map/reduce_scatter | solution.py:74
  1240.2 129.3 %reduce-scatter.17.cloned.1.call-start = ((), (), s32[]{:S(2)}) async-start(), calls=%async_computation.15 | async-start | bytes 294912 | tf_op jit(solution)/shard_map/reduce_scatter | solution.py:73
  1242.0 191.6 %reduce-scatter.23.cloned.1.call-start = ((), (), s32[]{:S(2)}) async-start(), calls=%async_computation.18 | async-start | bytes 294912 | tf_op jit(solution)/shard_map/reduce_scatter | solution.py:76
  1244.0 254.7 %reduce-scatter.21.cloned.1.call-start = ((), (), s32[]{:S(2)}) async-start(), calls=%async_computation.17 | async-start | bytes 589824 | tf_op jit(solution)/shard_map/reduce_scatter | solution.py:75
  1246.1 319.3 %reduce-scatter.15.cloned.1.call-start = ((), (), s32[]{:S(2)}) async-start(), calls=%async_computation.14 | async-start | bytes 884736 | tf_op jit(solution)/shard_map/reduce_scatter | solution.py:72
  1248.4 383.4 %reduce-scatter.25.cloned.1.call-start = ((), (), s32[]{:S(2)}) async-start(), calls=%async_computation.19 | async-start | bytes 1179648 | tf_op jit(solution)/shard_map/reduce_scatter | solution.py:77
  1249.2 449.5 %reduce-scatter.27.cloned.1.call-start = ((), (), s32[]{:S(2)}) async-start(), calls=%async_computation.20 | async-start | bytes 1179648 | tf_op jit(solution)/shard_map/reduce_scatter | solution.py:78
  (173 other events, 2961.0 us)
Sparse Core Ops, SparseCore 0:
  67.4 13.9 all-gather.11
  148.7 28.6 reduce-scatter.28
  179.0 16.7 all-gather.15
  197.3 16.7 all-gather.13
  287.5 31.3 reduce-scatter.30
  320.4 16.7 all-gather.17
  338.7 16.7 all-gather.19
  398.2 31.5 reduce-scatter.32
  434.8 16.7 all-gather.21
  475.7 31.3 reduce-scatter.34
  512.6 16.7 all-gather.23
  531.7 31.4 reduce-scatter.38
  565.9 31.4 reduce-scatter.40
  599.7 31.4 reduce-scatter.36
  669.7 13.0 all-gather.11
  751.0 27.7 reduce-scatter.28
  780.2 16.7 all-gather.15
  798.5 16.7 all-gather.13
  888.9 31.3 reduce-scatter.30
  921.7 16.7 all-gather.17
  940.0 16.7 all-gather.19
  999.5 31.5 reduce-scatter.32
  1036.1 16.7 all-gather.21
  1077.0 31.4 reduce-scatter.34
  1113.9 16.7 all-gather.23
  1133.0 31.4 reduce-scatter.38
  1167.0 31.4 reduce-scatter.40
  1201.0 31.4 reduce-scatter.36
Sparse Core Ops, SparseCore 1:
  1244.0 61.3 reduce-scatter.18
  1309.1 60.3 reduce-scatter.16
  1373.3 60.3 reduce-scatter.22
  1437.6 61.0 reduce-scatter.20
  1503.0 62.3 reduce-scatter.14
  1569.3 62.5 reduce-scatter.24
  1636.1 62.5 reduce-scatter.26
where the time goes:
time: 1710 us
  waiting for transfers between devices  795 us (46%)
  blocking collectives  527 us (31%)
  matrix products  166 us (10%)
  other arithmetic  91.1 us (5%)
  local copies, waits for them, and re-layouts  73.3 us (4%)
  loops' own time  36.5 us (2%)
    reduce_scatter x4, waiting for transfers between devices, input_grad(): lax.psum_scatter(grad_term(jnp.int32(0), own_rows * lax.axis_size('tensor...  117 us
    reduce_scatter x6, waiting for transfers between devices, branch_sum(): lax.psum_scatter(jnp.dot(mixture, weight, preferred_element_type=jnp.floa...  112 us
    all_gather x2, blocking collectives, gather_weights(): lax.all_gather(ffn_up, 'dp', axis=0, tiled=True)  67.2 us
    reduce_scatter x1, waiting for transfers between devices, reduce_grads(): lax.psum_scatter(grad_down, 'dp', scatter_dimension=1, tiled=True)  66.8 us
    reduce_scatter x1, waiting for transfers between devices, reduce_grads(): lax.psum_scatter(grad_qkv, 'dp', scatter_dimension=1, tiled=True)  66.6 us
    reduce_scatter x1, waiting for transfers between devices, reduce_grads(): lax.psum_scatter(grad_up, 'dp', scatter_dimension=0, tiled=True)  66.6 us
    reduce_scatter x1, waiting for transfers between devices, reduce_grads(): lax.psum_scatter(grad_pair, 'dp', scatter_dimension=1, tiled=True)  65 us
    reduce_scatter x1, waiting for transfers between devices, reduce_grads(): lax.psum_scatter(grad_cross, 'dp', scatter_dimension=1, tiled=True)  64.2 us
  transfers between devices with their start and end apart: 35, of which 23 were waited for; matrix products, arithmetic and copies ran while one was open for 9% of the time, Pallas kernels for 0%

commit v1 on v0

v1 whole, which is shorter than its diff:
```python
import functools

import jax
import jax.numpy as jnp
from jax import lax
from jax.experimental import pallas as pl
from jax.experimental.pallas import tpu as pltpu
from jax.sharding import PartitionSpec as P

DH = 64
LANES = 128
EPSILON = 1e-05
MASKED = -1e30
F32 = jnp.float32
BF16 = jnp.bfloat16
MESH = pl.DeviceIdType.MESH
HIGHEST = lax.Precision.HIGHEST


def nn(a, b):
    return lax.dot_general(a, b, (((1,), (0,)), ((), ())), preferred_element_type=F32)


def nt(a, b):
    return lax.dot_general(a, b, (((1,), (1,)), ((), ())), preferred_element_type=F32)


def normalize(values):
    center = values - jnp.mean(values, axis=-1, keepdims=True)
    spread = jnp.mean(center * center, axis=-1, keepdims=True)
    inv = lax.rsqrt(spread + EPSILON)
    return center * inv, inv


def norm_grad(values, grad, gain):
    xhat, inv = normalize(values)
    e = grad * gain
    back = inv * (
        e
        - jnp.mean(e, axis=-1, keepdims=True)
        - xhat * jnp.mean(e * xhat, axis=-1, keepdims=True)
    )
    return (
        back,
        jnp.sum(grad * xhat, axis=0, keepdims=True),
        jnp.sum(grad, axis=0, keepdims=True),
    )


def gelu_both(v):
    c = 0.7978845608028654
    v2 = v * v
    t = jnp.tanh(v * (c + (c * 0.044715) * v2))
    half = 0.5 * (1.0 + t)
    slope = half + (0.5 * v) * (1.0 - t * t) * (c + (3.0 * c * 0.044715) * v2)
    return v * half, slope


def layer_kernel(cfg, *refs):
    fused, nz, ny, rb, own, wide, nf = cfg
    rows_all = 4 * own
    nseg = 8 + 2 * nf
    gseg = nseg
    refs = list(refs)

    def take(count):
        got, refs[:count] = refs[:count], []
        return got

    x_ref, m_ref, c_ref, tl_ref, sl_ref = take(5)
    if fused:
        wqkv_ref, wo_ref, cq_ref, ckv_ref, co_ref, up_ref, dn_ref = take(7)
        gain_refs = take(6)
    else:
        wfull_ref, gfull_ref = take(2)
    out_ref, gi_ref, gm_ref, gw_ref = take(4)
    (xs, ms, cs, wg, gains, n1, n2, n3, h1, h2, gh, gb16, qs, ks, vs, cqs, cks, cvs,
     vt, smix, cmix, slse, clse, act, gbf, dm, dq, dka, dva, dk, dv, ps, pr, ys, yr,
     us, ur, outs, osend, gis, gisend, gms, gmsend, gs, bias, gacc) = take(46)
    if fused:
        pack, gz, gy, rx, hx, ry, hy, rz = take(8)
    ssem, rsem, xss, xrs, lsem = take(5)

    p = lax.axis_index("tensor") // 2
    c = lax.axis_index("tensor") % 2
    t = 2 * p + c
    tx = 2 * (1 - p) + c
    dp_at = lax.axis_index("dp")
    core_peer = {"dp": dp_at, "tensor": 2 * p + 1 - c}
    x_peer = {"dp": dp_at, "tensor": tx}
    z = dp_at // ny
    y = dp_at % ny
    y_peer = {"dp": z * ny + (1 - y), "tensor": t}

    def z_peer(k):
        return {"dp": ((z + k) % nz) * ny + y, "tensor": t}

    counter = [0]
    sent = []

    def push(src, dst, peer):
        i = counter[0]
        counter[0] += 1
        cp = pltpu.make_async_remote_copy(
            src, dst, ssem.at[i], rsem.at[i], device_id=peer, device_id_type=MESH
        )
        cp.start()
        sent.append(cp)
        return cp

    lcount = [0]
    local_open = []

    def local(src, dst):
        cp = pltpu.make_async_copy(src, dst, lsem.at[lcount[0]])
        lcount[0] += 1
        cp.start()
        return cp

    def rows(j, size=own):
        return pl.ds(pl.multiple_of(j * size, size), size)

    peers = [core_peer, x_peer]
    if fused:
        if ny > 1:
            peers.append(y_peer)
        peers += [z_peer(k) for k in range(1, nz)]
    barrier = pltpu.get_barrier_semaphore()
    for peer in peers:
        pl.semaphore_signal(barrier, inc=1, device_id=peer, device_id_type=MESH)
    pl.semaphore_wait(barrier, len(peers))

    def spread(src, buf):
        over = push(src.at[1 - p], buf.at[rows(t)], x_peer)
        keep = local(src.at[p], buf.at[rows(t)])
        near = push(src.at[p], buf.at[rows(t)], core_peer)
        return over, keep, near

    def settle(src_copies, buf):
        over, keep, near = src_copies
        over.wait_recv()
        relay = push(buf.at[rows(tx)], buf.at[rows(tx)], core_peer)
        keep.wait()
        near.wait_recv()
        return relay

    half = pl.ds(pl.multiple_of(p * LANES, LANES), LANES)
    other_half = pl.ds(pl.multiple_of((1 - p) * LANES, LANES), LANES)

    def gather_one(lo, hi):
        return [
            push(pack.at[lo:hi], wg.at[lo:hi, z, y, :, half], z_peer(k)) for k in range(1, nz)
        ]

    def gather_two(lo, hi, prior):
        for cp in prior:
            cp.wait_recv()
        if ny == 1:
            return []
        part = wg.at[lo:hi, :, y, :, half]
        return [push(part, part, y_peer)]

    def gather_three(lo, hi, prior):
        for cp in prior:
            cp.wait_recv()
        part = wg.at[lo:hi, :, :, :, half]
        return [push(part, part, x_peer)]

    def weight(s):
        return wg[s].reshape(nz * ny * rb, 2 * LANES)

    xin = spread(x_ref, xs)
    if fused:
        eye = (
            lax.broadcasted_iota(jnp.int32, (rb, rb), 0)
            == lax.broadcasted_iota(jnp.int32, (rb, rb), 1)
        ).astype(BF16)
        pack[0:3] = wqkv_ref[...]
        pack[3] = nt(eye, wo_ref[...]).astype(BF16)
        pack[4] = cq_ref[...]
        pack[5:7] = ckv_ref[...]
        pack[7] = nt(eye, co_ref[...]).astype(BF16)
        ga = gather_one(0, 3)
        place = (
            lax.broadcasted_iota(jnp.int32, (rb, wide), 0) + dp_at * rb
            == lax.broadcasted_iota(jnp.int32, (rb, wide), 1)
        ).astype(BF16)
        gz[0] = jnp.zeros((16, wide), BF16)
        for i in range(6):
            gz[0, i : i + 1, :] = nn(gain_refs[i][...], place).astype(BF16)
        gcp = [push(gz.at[0], gz.at[k], z_peer(k)) for k in range(1, nz)]
        for i in range(nf):
            pack[8 + i] = up_ref[:, i * LANES : (i + 1) * LANES]
            pack[8 + nf + i] = nt(eye, dn_ref[i * LANES : (i + 1) * LANES, :]).astype(BF16)
        wg[:, z, y, :, half] = pack[...]
        for cp in gcp:
            cp.wait_recv()
        total = gz[0].astype(F32)
        for k in range(1, nz):
            total = total + gz[k].astype(F32)
        if ny > 1:
            gy[0] = total.astype(BF16)
            gcp = push(gy.at[0], gy.at[1], y_peer)
            gcp.wait_recv()
            total = total + gy[1].astype(F32)
        gains[...] = total
        ga = gather_two(0, 3, ga)
        go = gather_one(3, 4)
        gb = gather_one(4, 8)
    else:
        wcp = local(wfull_ref, wg)
        gains[...] = gfull_ref[...]
        wcp.wait()
    min_ = spread(m_ref, ms)
    cin = spread(c_ref, cs)

    relay = settle(xin, xs)
    relay.wait_recv()

    sub = min(64, own)
    per = own // sub
    gacc[...] = jnp.zeros_like(gacc)

    def norm_rows(i, _):
        r = rows(i, sub)
        xhat, _unused = normalize(xs[r, :].astype(F32))
        n1[r, :] = (xhat * gains[0:1, :] + gains[1:2, :]).astype(BF16)
        return 0

    lax.fori_loop(0, 4 * per, norm_rows, 0)

    if fused:
        ga = gather_three(0, 3, ga)
        go = gather_two(3, 4, go)
        gb = gather_two(4, 8, gb)
        gc = gather_one(8, nseg)
        for cp in ga:
            cp.wait_recv()

    def put_pairs(buf, r, value):
        v = value.astype(BF16)
        buf[0, r, :] = v[:, :LANES]
        buf[1, r, :] = v[:, LANES:]

    def pairs(buf, r):
        return jnp.concatenate([buf[0, r, :], buf[1, r, :]], axis=1)

    scale = DH ** (-0.5)

    def put_transposed(buf, r, value):
        vt_ = value.T.astype(BF16)
        buf[0, :, r] = vt_[:LANES]
        buf[1, :, r] = vt_[LANES:]

    def project(j, _):
        r = rows(j)
        rowsv = n1[r, :]
        put_pairs(qs, r, nn(rowsv, weight(0)).astype(BF16) * jnp.asarray(scale, BF16))
        put_pairs(ks, r, nn(rowsv, weight(1)))
        val = nn(rowsv, weight(2))
        put_pairs(vs, r, val)
        put_transposed(vt, r, val.astype(BF16).astype(F32))
        return 0

    lax.fori_loop(0, 4, project, 0)

    if fused:
        go = gather_three(3, 4, go)
        gb = gather_three(4, 8, gb)
        gc = gather_two(8, nseg, gc)

    def only(value, u):
        lane = lax.broadcasted_iota(jnp.int32, value.shape, 1)
        keep = (lane // DH) == u
        return jnp.where(keep, value, jnp.zeros_like(value))

    def causal_mask(scores, keys):
        tail = scores[keys - own :]
        key_at = lax.broadcasted_iota(jnp.int32, tail.shape, 0)
        query_at = lax.broadcasted_iota(jnp.int32, tail.shape, 1)
        tail = jnp.where(key_at <= query_at, tail, MASKED)
        if keys == own:
            return tail
        return jnp.concatenate([scores[: keys - own], tail], axis=0)

    def masked(scores, keys, causal):
        if causal:
            return causal_mask(scores, keys)
        b = bias[...]
        return scores + jnp.concatenate([b] * (own // LANES), axis=1)

    def attend(q_s, k_s, v_t, mix, lse, r, keys, causal):
        def pair(pp, _):
            q = q_s[pp, r, :]
            k = k_s[pp, 0:keys, :]
            parts = []
            for u in range(2):
                s = masked(nt(only(k, u), q), keys, causal)
                top = jnp.max(s, axis=0, keepdims=True)
                e = jnp.exp(s - top)
                total = jnp.sum(e, axis=0, keepdims=True)
                o = nn(v_t[pp, u * DH : (u + 1) * DH, 0:keys], e.astype(BF16))
                parts.append(o * (1.0 / total))
                lse[2 * pp + u, :, r] = top + jnp.log(total)
            mix[pp, r, :] = jnp.concatenate(parts, axis=0).T.astype(BF16)
            return 0

        lax.fori_loop(0, 2, pair, 0)

    def exchange(point, j):
        b = point % 2
        i = point * 4 + j
        return pltpu.make_async_remote_copy(
            ps.at[b, rows(j)], pr.at[b, rows(j)], xss.at[i], xrs.at[i],
            device_id=core_peer, device_id_type=MESH,
        )

    def send_sum(point, j, value):
        ps[point % 2, rows(j), :] = value.astype(BF16)
        exchange(point, j).start()

    def summed(point, r):
        b = point % 2
        return ps[b, r, :].astype(F32) + pr[b, r, :].astype(F32)

    for j in range(4):
        r = rows(j)
        attend(qs, ks, vt, smix, slse, r, own * (j + 1), True)
        if fused and j == 0:
            for cp in go:
                cp.wait_recv()
        send_sum(0, j, nt(pairs(smix, r), weight(3)))
        if j == 1:
            mrelay = settle(min_, ms)

    if fused:
        for cp in gb:
            cp.wait_recv()
        gc = gather_three(8, nseg, gc)
    mrelay.wait_recv()

    key_at = lax.broadcasted_iota(jnp.int32, (rows_all, LANES), 0)
    bias[...] = jnp.where(key_at < sl_ref[p], 0.0, MASKED)

    def project_cross(j, _):
        r = rows(j)
        rowsv = ms[r, :]
        put_pairs(cks, r, nn(rowsv, weight(5)))
        val = nn(rowsv, weight(6))
        put_pairs(cvs, r, val)
        put_transposed(vt, r, val.astype(BF16).astype(F32))
        return 0

    lax.fori_loop(0, 4, project_cross, 0)

    def second(j, _):
        exchange(0, j).wait_recv()
        exchange(0, j).wait_send()

        def part(i, _):
            r = rows(j * per + i, sub)
            h = xs[r, :].astype(F32) + summed(0, r)
            h1[r, :] = h
            xhat, _unused = normalize(h)
            n2[r, :] = (xhat * gains[2:3, :] + gains[3:4, :]).astype(BF16)
            return 0

        lax.fori_loop(0, per, part, 0)
        r = rows(j)
        put_pairs(cqs, r, nn(n2[r, :], weight(4)).astype(BF16) * jnp.asarray(scale, BF16))
        return 0

    lax.fori_loop(0, 4, second, 0)

    def cross_block(j, _):
        r = rows(j)
        attend(cqs, cks, vt, cmix, clse, r, rows_all, False)
        send_sum(1, j, nt(pairs(cmix, r), weight(7)))
        return 0

    lax.fori_loop(0, 4, cross_block, 0)
    crelay = settle(cin, cs)
    crelay.wait_recv()
    if fused:
        for cp in gc:
            cp.wait_recv()

    limit = tl_ref[p]

    def live(r_first, size):
        at = lax.broadcasted_iota(jnp.int32, (size, wide), 0) + r_first
        return at < limit

    def third(j, _):
        exchange(1, j).wait_recv()
        exchange(1, j).wait_send()

        def part(i, _):
            r = rows(j * per + i, sub)
            h = h1[r, :] + summed(1, r)
            h2[r, :] = h
            xhat, _unused = normalize(h)
            n3[r, :] = (xhat * gains[4:5, :] + gains[5:6, :]).astype(BF16)
            first = (j * per + i) * sub
            cot = cs[r, :]
            gb16[r, :] = jnp.where(live(first, sub), cot, jnp.zeros_like(cot))
            return 0

        lax.fori_loop(0, per, part, 0)
        r = rows(j)
        rowsv = n3[r, :]
        cot = gb16[r, :]
        for s in range(nf):
            before = nn(rowsv, weight(8 + s))
            active, slope = gelu_both(before)
            act[s, r, :] = active.astype(BF16)
            gbf[s, r, :] = (nn(cot, weight(8 + nf + s)) * slope).astype(BF16)
        back = nt(gbf[0, r, :], weight(8))
        for s in range(1, nf):
            back = back + nt(gbf[s, r, :], weight(8 + s))
        send_sum(2, j, back)
        val = nt(act[0, r, :], weight(8 + nf))
        for s in range(1, nf):
            val = val + nt(act[s, r, :], weight(8 + nf + s))
        ys[r, :] = val.astype(BF16)
        return 0

    lax.fori_loop(0, 4, third, 0)

    ycp = [
        push(ys.at[rows(2 * k + 1 - c)], yr.at[k], core_peer) for k in range(2)
    ]

    def weight_grads(a_buf, items):
        chunk = ny * rb
        for zi in range(nz):
            at = a_buf[:, zi * chunk : (zi + 1) * chunk].T
            for s, load in items:
                gs[s, zi] = nn(at, load()).astype(BF16).reshape(ny, rb, 2 * LANES)

    every = pl.ds(0, rows_all)

    def whole(buf):
        return lambda: pairs(buf, every)

    def plane(buf, s):
        return lambda: buf[s]

    weight_grads(gb16, [(8 + nf + s, plane(act, s)) for s in range(nf)])
    weight_grads(n3, [(8 + s, plane(gbf, s)) for s in range(nf)])

    def reduce_one(lo, hi):
        return push(gs.at[lo:hi, :, :, :, other_half], rx.at[lo:hi], x_peer)

    def reduce_two(lo, hi, prior):
        prior.wait_recv()
        def one(s, _):
            mine = gs[s, :, :, :, half].astype(F32)
            hx[s] = (mine + rx[s].astype(F32)).astype(BF16)
            return 0
        lax.fori_loop(lo, hi, one, 0)
        if ny == 1:
            return None
        return push(hx.at[lo:hi, :, 1 - y], ry.at[lo:hi], y_peer)

    def reduce_three(lo, hi, prior):
        if prior is not None:
            prior.wait_recv()
        def one(s, _):
            v = hx[s, :, y].astype(F32)
            if ny > 1:
                v = v + ry[s].astype(F32)
            hy[s] = v.astype(BF16)
            return 0
        lax.fori_loop(lo, hi, one, 0)
        return [
            push(hy.at[lo:hi, (z + k) % nz], rz.at[k - 1, lo:hi], z_peer(k))
            for k in range(1, nz)
        ]

    def reduce_done(lo, hi, prior):
        for cp in prior:
            cp.wait_recv()
        def one(s, _):
            v = hy[s, z].astype(F32)
            for k in range(1, nz):
                v = v + rz[k - 1, s].astype(F32)
            gw_ref[s] = v
            return 0
        lax.fori_loop(lo, hi, one, 0)

    if fused:
        rf = reduce_one(8, nseg)

    def finish_rows(k, dst):
        def part(i, _):
            r = rows((2 * k + c) * per + i, sub)
            q = rows(i, sub)
            val = h2[r, :] + ys[r, :].astype(F32) + yr[k, q, :].astype(F32)
            keep = live(((2 * k + c) * per + i) * sub, sub)
            dst[q, :] = jnp.where(keep, val, 0.0).astype(BF16)
            return 0
        lax.fori_loop(0, per, part, 0)

    for cp in ycp:
        cp.wait_recv()
    finish_rows(1 - p, osend)
    ocp = push(osend, outs.at[p], x_peer)
    finish_rows(p, outs.at[p])

    def back_three(j, _):
        exchange(2, j).wait_recv()
        exchange(2, j).wait_send()

        def part(i, _):
            r = rows(j * per + i, sub)
            dx, dgain, dbias = norm_grad(h2[r, :], summed(2, r), gains[4:5, :])
            gacc[4:5, :] += dgain
            gacc[5:6, :] += dbias
            g = gb16[r, :].astype(F32) + dx
            gh[r, :] = g
            gb16[r, :] = g.astype(BF16)
            return 0

        return lax.fori_loop(0, per, part, 0)

    lax.fori_loop(0, 4, back_three, 0)

    if fused:
        rf = reduce_two(8, nseg, rf)

    sel_row = lax.broadcasted_iota(jnp.int32, (8, LANES), 0)
    sel_lane = lax.broadcasted_iota(jnp.int32, (8, LANES), 1)
    selector = (sel_lane // DH == sel_row).astype(F32)

    def attend_back(q_s, k_s, kt, v_s, mix, lse, r, keys, causal):
        def pair(pp, _):
            q = q_s[pp, r, :]
            k = k_s[pp, 0:keys, :]
            v = v_s[pp, 0:keys, :]
            do = dm[pp, r, :]
            prod = do.astype(F32) * mix[pp, r, :].astype(F32)
            delta = lax.dot_general(
                selector, prod, (((1,), (1,)), ((), ())),
                precision=HIGHEST, preferred_element_type=F32,
            )
            parts = []
            dvp = None
            for u in range(2):
                s = masked(nt(only(k, u), q), keys, causal)
                e = jnp.exp(s - lse[2 * pp + u, :, r])
                d = nt(only(v, u), do)
                ds = (e * (d - delta[u : u + 1])).astype(BF16)
                dv_u = nn(e.astype(BF16), only(do, u))
                dk_u = nn(ds, only(q, u))
                dvp = dv_u if dvp is None else dvp + dv_u
                dkp = dk_u if u == 0 else dkp + dk_u
                parts.append(nn(kt[pp, u * DH : (u + 1) * DH, 0:keys], ds) * scale)
            dka[pp, 0:keys, :] += dkp
            dva[pp, 0:keys, :] += dvp
            dq[pp, r, :] = jnp.concatenate(parts, axis=0).T.astype(BF16)
            return 0

        lax.fori_loop(0, 2, pair, 0)

    def transpose_keys(buf):
        def one(j, _):
            r = rows(j)
            for pp in range(2):
                vt[pp, :, r] = buf[pp, r, :].astype(F32).T.astype(BF16)
            return 0
        lax.fori_loop(0, 4, one, 0)

    transpose_keys(cks)
    dka[...] = jnp.zeros_like(dka)
    dva[...] = jnp.zeros_like(dva)

    def cross_back(j, _):
        r = rows(j)
        put_pairs(dm, r, nn(gb16[r, :], weight(7)))
        attend_back(cqs, cks, vt, cvs, cmix, clse, r, rows_all, False)
        send_sum(3, j, nt(pairs(dq, r), weight(4)))
        return 0

    lax.fori_loop(0, 4, cross_back, 0)
    if fused:
        rf = reduce_three(8, nseg, rf)

    def cross_back_keys(j, _):
        r = rows(j)
        for pp in range(2):
            dk[pp, r, :] = dka[pp, r, :].astype(BF16)
            dv[pp, r, :] = dva[pp, r, :].astype(BF16)
        val = nt(pairs(dk, r), weight(5)) + nt(pairs(dv, r), weight(6))
        us[r, :] = val.astype(BF16)
        return 0

    lax.fori_loop(0, 4, cross_back_keys, 0)
    ucp = [
        push(us.at[rows(2 * k + 1 - c)], ur.at[k], core_peer) for k in range(2)
    ]
    weight_grads(gb16, [(7, whole(cmix))])
    weight_grads(n2, [(4, whole(dq))])
    weight_grads(ms, [(5, whole(dk)), (6, whole(dv))])

    def memory_rows(k, dst):
        def part(i, _):
            r = rows((2 * k + c) * per + i, sub)
            q = rows(i, sub)
            dst[q, :] = (us[r, :].astype(F32) + ur[k, q, :].astype(F32)).astype(BF16)
            return 0
        lax.fori_loop(0, per, part, 0)

    for cp in ucp:
        cp.wait_recv()
    memory_rows(1 - p, gmsend)
    mcp = push(gmsend, gms.at[p], x_peer)
    memory_rows(p, gms.at[p])

    def back_two(j, _):
        exchange(3, j).wait_recv()
        exchange(3, j).wait_send()

        def part(i, _):
            r = rows(j * per + i, sub)
            dx, dgain, dbias = norm_grad(h1[r, :], summed(3, r), gains[2:3, :])
            gacc[2:3, :] += dgain
            gacc[3:4, :] += dbias
            g = gh[r, :] + dx
            gh[r, :] = g
            gb16[r, :] = g.astype(BF16)
            return 0

        return lax.fori_loop(0, per, part, 0)

    lax.fori_loop(0, 4, back_two, 0)
    weight_grads(gb16, [(3, whole(smix))])
    if fused:
        reduce_done(8, nseg, rf)
        rc = reduce_one(3, 8)

    transpose_keys(ks)
    dka[...] = jnp.zeros_like(dka)
    dva[...] = jnp.zeros_like(dva)
    for j in reversed(range(4)):
        r = rows(j)
        put_pairs(dm, r, nn(gb16[r, :], weight(3)))
        attend_back(qs, ks, vt, vs, smix, slse, r, own * (j + 1), True)
        for pp in range(2):
            dk[pp, r, :] = dka[pp, r, :].astype(BF16)
            dv[pp, r, :] = dva[pp, r, :].astype(BF16)
        val = nt(pairs(dq, r), weight(0)) + nt(pairs(dk, r), weight(1))
        send_sum(4, j, val + nt(pairs(dv, r), weight(2)))
        if fused and j == 3:
            rc = reduce_two(3, 8, rc)
        if fused and j == 2:
            rc = reduce_three(3, 8, rc)

    weight_grads(n1, [(0, whole(dq)), (1, whole(dk)), (2, whole(dv))])
    if fused:
        rt = reduce_one(0, 3)
        reduce_done(3, 8, rc)

    def back_one(k, j, dst):
        exchange(4, j).wait_recv()

        def part(i, _):
            r = rows(j * per + i, sub)
            q = rows(i, sub)
            dx, dgain, dbias = norm_grad(xs[r, :].astype(F32), summed(4, r), gains[0:1, :])
            gacc[0:1, :] += dgain
            gacc[1:2, :] += dbias
            if dst is not None:
                dst[q, :] = (gh[r, :] + dx).astype(BF16)
            return 0

        lax.fori_loop(0, per, part, 0)

    back_one(0, tx, gisend)
    icp = push(gisend, gis.at[p], x_peer)
    back_one(0, t, gis.at[p])
    back_one(0, 2 * p + 1 - c, None)
    back_one(0, 2 * (1 - p) + 1 - c, None)
    for j in range(4):
        exchange(4, j).wait_send()

    spread_rows = jnp.concatenate(
        [gacc[...], jnp.zeros((LANES - 8, wide), F32)], axis=0
    )
    columns = spread_rows.T.astype(BF16)
    gs[gseg] = jnp.concatenate([columns, columns], axis=1).reshape(nz, ny, rb, 2 * LANES)

    if fused:
        rg = reduce_one(gseg, gseg + 1)
        rt = reduce_two(0, 3, rt)
        rg = reduce_two(gseg, gseg + 1, rg)
        rt = reduce_three(0, 3, rt)
        rg = reduce_three(gseg, gseg + 1, rg)
        reduce_done(0, 3, rt)
        reduce_done(gseg, gseg + 1, rg)
    else:
        last = [local(gs, gw_ref)]

    ocp.wait_recv()
    mcp.wait_recv()
    icp.wait_recv()
    finals = [local(outs, out_ref), local(gms, gm_ref), local(gis, gi_ref)]
    if not fused:
        finals += last
    for cp in finals:
        cp.wait()
    for cp in sent:
        cp.wait_send()


def body(ndp, inputs, memory, tgt_len, src_len, cotangent, w_qkv, w_out, cross_query, cross_kv,
         cross_out, ffn_up, ffn_down, *gain_list):
    own, wide = inputs.shape[1], inputs.shape[2]
    rb = w_qkv.shape[1]
    nf = ffn_up.shape[1] // LANES
    nseg = 8 + 2 * nf
    rows_all = 4 * own
    fused = rb % 16 == 0
    if fused:
        ny = 2 if ndp % 2 == 0 else 1
        nz = ndp // ny
        block = rb
    else:
        ny, nz, block = 1, 1, wide
    cfg = (fused, nz, ny, block, own, wide, nf)

    any_spec = pl.BlockSpec(memory_space=pl.ANY)
    smem = pl.BlockSpec(memory_space=pltpu.SMEM)
    vmem = pl.BlockSpec(memory_space=pltpu.VMEM)
    operands = [inputs, memory, cotangent, tgt_len, src_len]
    specs = [any_spec] * 3 + [smem] * 2
    if fused:
        weights = [w_qkv, w_out, cross_query, cross_kv, cross_out, ffn_up, ffn_down]
        weights += [g[None, :] for g in gain_list]
        operands += weights
        specs += [vmem] * len(weights)
    else:
        pieces = [w_qkv, w_out.T[None], cross_query[None], cross_kv, cross_out.T[None]]
        pieces += [ffn_up.reshape(rb, nf, LANES).swapaxes(0, 1)]
        pieces += [ffn_down.reshape(nf, LANES, rb).swapaxes(1, 2)]
        packed = lax.all_gather(jnp.concatenate(pieces, axis=0), "dp", axis=1, tiled=True)
        index = lax.axis_index("tensor")
        flipped = lax.ppermute(packed, "tensor", [(i, (i + 2) % 4) for i in range(4)])
        low = jnp.where(index < 2, packed, flipped)
        high = jnp.where(index < 2, flipped, packed)
        full = jnp.concatenate([low, high], axis=2)[:, None, None]
        gathered = lax.all_gather(jnp.stack(gain_list), "dp", axis=1, tiled=True)
        operands += [full, jnp.pad(gathered.astype(F32), ((0, 10), (0, 0)))]
        specs += [any_spec, vmem]

    bf = lambda *shape: pltpu.VMEM(shape, BF16)
    fl = lambda *shape: pltpu.VMEM(shape, F32)
    seq = (rows_all, wide)
    heads = (2, rows_all, LANES)
    scratch = [
        bf(*seq), bf(*seq), bf(*seq), bf(nseg, nz, ny, block, 2 * LANES), fl(16, wide),
        bf(*seq), bf(*seq), bf(*seq), fl(*seq), fl(*seq), fl(*seq), bf(*seq),
        bf(*heads), bf(*heads), bf(*heads), bf(*heads), bf(*heads), bf(*heads),
        bf(2, LANES, rows_all), bf(*heads), bf(*heads), fl(4, 1, rows_all), fl(4, 1, rows_all),
        bf(nf, rows_all, 2 * LANES), bf(nf, rows_all, 2 * LANES),
        bf(*heads), bf(*heads), fl(*heads), fl(*heads), bf(*heads), bf(*heads),
        bf(2, *seq), bf(2, *seq), bf(*seq), bf(2, own, wide), bf(*seq), bf(2, own, wide),
        bf(2, own, wide), bf(own, wide), bf(2, own, wide), bf(own, wide),
        bf(2, own, wide), bf(own, wide),
        bf(nseg + 1, nz, ny, block, 2 * LANES), fl(rows_all, LANES), fl(8, wide),
    ]
    if fused:
        scratch += [
            bf(nseg, block, LANES), bf(nz, 16, wide), bf(2, 16, wide),
            bf(nseg + 1, nz, ny, block, LANES), bf(nseg + 1, nz, ny, block, LANES),
            bf(nseg + 1, nz, block, LANES), bf(nseg + 1, nz, block, LANES),
            bf(max(nz - 1, 1), nseg + 1, block, LANES),
        ]
    dma = pltpu.SemaphoreType.DMA
    scratch += [dma((96,)), dma((96,)), dma((20,)), dma((20,)), dma((12,))]

    if fused:
        grads_shape = jax.ShapeDtypeStruct((nseg + 1, block, LANES), F32)
        grads_spec = vmem
    else:
        grads_shape = jax.ShapeDtypeStruct((nseg + 1, nz, ny, block, 2 * LANES), BF16)
        grads_spec = any_spec
    act_shape = jax.ShapeDtypeStruct(inputs.shape, BF16)
    output, grad_in, grad_mem, grads = pl.pallas_call(
        functools.partial(layer_kernel, cfg),
        out_shape=(act_shape, act_shape, act_shape, grads_shape),
        in_specs=specs,
        out_specs=(any_spec, any_spec, any_spec, grads_spec),
        scratch_shapes=scratch,
        compiler_params=pltpu.CompilerParams(
            collective_id=0, has_side_effects=True, vmem_limit_bytes=62 << 20
        ),
        name="layer",
    )(*operands)

    if not fused:
        mine = grads[:, 0, 0].astype(F32)
        index = lax.axis_index("tensor")
        low, high = mine[:, :, :LANES], mine[:, :, LANES:]
        keep = jnp.where(index < 2, low, high)
        give = jnp.where(index < 2, high, low)
        keep = keep + lax.ppermute(give, "tensor", [(i, (i + 2) % 4) for i in range(4)])
        grads = lax.psum_scatter(keep, "dp", scatter_dimension=1, tiled=True)

    def merge(blocks):
        return jnp.swapaxes(blocks, 0, 1).reshape(blocks.shape[1], -1)

    gain_grads = grads[nseg][:, :6].T
    return (
        output,
        grad_in.astype(F32),
        grad_mem.astype(F32),
        grads[0:3],
        grads[3].T,
        grads[4],
        grads[5:7],
        grads[7].T,
        merge(grads[8 : 8 + nf]),
        merge(grads[8 + nf : nseg]).T,
        gain_grads[0],
        gain_grads[1],
        gain_grads[2],
        gain_grads[3],
        gain_grads[4],
        gain_grads[5],
    )


def solution(mesh):
    return jax.shard_map(
        functools.partial(body, mesh.shape["dp"]),
        mesh=mesh,
        in_specs=(
            P("dp", "tensor", None),
            P("dp", "tensor", None),
            P("dp"),
            P("dp"),
            P("dp", "tensor", None),
            P(None, "dp", "tensor"),
            P("tensor", "dp"),
            P("dp", "tensor"),
            P(None, "dp", "tensor"),
            P("tensor", "dp"),
            P("dp", "tensor"),
            P("tensor", "dp"),
            P("dp"),
            P("dp"),
            P("dp"),
            P("dp"),
            P("dp"),
            P("dp"),
        ),
        out_specs=(
            P("dp", "tensor", None),
            P("dp", "tensor", None),
            P("dp", "tensor", None),
            P(None, "dp", "tensor"),
            P("tensor", "dp"),
            P("dp", "tensor"),
            P(None, "dp", "tensor"),
            P("tensor", "dp"),
            P("dp", "tensor"),
            P("tensor", "dp"),
            P("dp"),
            P("dp"),
            P("dp"),
            P("dp"),
            P("dp"),
            P("dp"),
        ),
        check_vma=False,
    )
```

time: 1710 us -> 218 us (0.13)
  waiting for transfers between devices: 795 us -> 0 us
  blocking collectives: 527 us -> 0 us
  Pallas kernels: 0 us -> 203 us
  matrix products: 166 us -> 0 us
  other arithmetic: 91.1 us -> 2.2 us
  local copies, waits for them, and re-layouts: 73.3 us -> 11.4 us
  loops' own time: 36.5 us -> 0 us
    reduce_scatter x21 -> x0, waiting for transfers between devices: 741 us -> none  [the longest x4 117 us: input_grad(): lax.psum_scatter(grad_term(jnp.int32(0), own_rows * lax.axis_size('tensor...]
    all_gather x14 -> x0, blocking collectives: 437 us -> none  [the longest x2 67.2 us: gather_weights(): lax.all_gather(ffn_up, 'dp', axis=0, tiled=True)]
    pallas_call x0 -> x1, Pallas kernels: none -> 203 us  [body(): pl.pallas_call(functools.partial(layer_kernel, cfg), out_shape=(act_shape...]
    dot_general x98 -> x0, matrix products: 166 us -> none  [the longest x8 15.1 us: one_block(): jnp.einsum('hqk,qhd->khd', probs.astype(jnp.bfloat16), grad_block, prefer...]
    all_gather x14 -> x0, waiting for transfers between devices: 51.7 us -> none  [the longest x6 51.6 us: grad_rows(): return lax.all_gather(own_part, 'tensor', axis=0, tiled=True)]
    while x2 -> x0, blocking collectives: 46.1 us -> none
    while x437 -> x0, local copies, waits for them, and re-layouts: 44.7 us -> none
    unnamed x1 -> x0, blocking collectives: 37.1 us -> none
  transfers between devices with their start and end apart: 35 -> 0, of which waited for: 23 -> 0; matrix products, arithmetic and copies ran while one was open for 9% -> 0% of each run, Pallas kernels for 0% -> 0%
where the time goes in v1:
time: 218 us
  Pallas kernels  203 us (93%)
  local copies, waits for them, and re-layouts  11.4 us (5%)
  other arithmetic  2.2 us (1%)
    pallas_call x1, Pallas kernels, body(): pl.pallas_call(functools.partial(layer_kernel, cfg), out_shape=(act_shape...  203 us
    unnamed x13, local copies, waits for them, and re-layouts  5.45 us

profile of v1, /device:TPU:0, one launch (start us, length us, event | category | flops | bytes accessed | tf_op | source)
XLA Modules:
  0.0 217.6 jit_solution(17975301075965078001)
XLA Ops:
  0.6 0.0 copy-start.3
  0.7 1.5 copy.37.refs_6_
  2.1 1.4 copy.38.refs_9_
  3.6 0.0 copy-done.3
  3.6 0.8 copy.39.refs_11_
  4.3 203.3 %layer.1 = (bf16[2,256,512]{2,1,0:T(8,128)(2,1)}, bf16[2,256,512]{2,1,0:T(8,128)(2,1)}, bf16[2,256,512]{2,1,0:T(8,128)(2,1)}, f32[17,64,128]{2,1,0:T(8,128)}) custom-call(bf16[2,256,512]{2,1,0:T(8,128)(2,1)} %refs_0_.1, bf16[2,256,512]{2,1,0:T(8,128)(2,1)} %refs_1_.1, bf16[2,256,512]{2,1,0:T(8,128)(2,1)} %refs_2_.1, s32[2]{0:T(128)} %refs_3_.1, s32[2]{0:T(128)} %refs_4_.1, ...), custom_call_target="tpu_custom_call" | custom-call | tf_op jit(solution)/shard_map/layer/pallas_call | solution.py:789
  207.6 1.5 slice.48
  209.1 1.5 slice.45
  210.6 1.4 slice_bitcast_fusion.3
  212.1 1.0 slice_bitcast_fusion
  213.0 0.0 copy-start.1
  213.1 0.8 slice_reduce_fusion
  213.9 0.7 bitcast_bitcast_fusion
  214.6 0.0 copy-done.1
  214.6 0.0 copy-start
  214.6 1.1 convert_element_type.6
  215.7 0.0 copy-done
  215.7 0.0 copy-start.2
  215.7 1.1 convert_element_type.7
  216.8 0.0 copy-done.2
  216.8 0.8 copy.47
  (1 shorter events, 0.0 us)
Async XLA Ops:
  0.6 2.9 %copy-start.3 = (bf16[512,64]{0,1:T(8,128)(2,1)S(1)}, bf16[512,64]{0,1:T(8,128)(2,1)}, u32[]{:S(2)}) copy-start(bf16[512,64]{0,1:T(8,128)(2,1)} %param.29) | copy-start | bytes 196612
  213.0 1.5 copy-start.1
  214.6 1.1 copy-start
  215.7 1.1 copy-start.2

commit v2 on v1

--- a/solution.py
+++ b/solution.py
@@ -56,11 +56,25 @@
     return v * half, slope
 
 
+SUMS = (("xyz", 5), ("yxz", 5), ("yzx", 5))
+
+
+def sum_shapes(order, segs, nz, ny, rows):
+    shapes, left = [], {"x": 2 * LANES, "y": (ny,), "z": (nz,)}
+    for i, axis in enumerate(order):
+        left[axis] = LANES if axis == "x" else ()
+        shape = (segs, *left["z"], *left["y"], rows, left["x"])
+        shapes.append((nz - 1, *shape) if axis == "z" else shape)
+        if i < 2:
+            shapes.append(shape)
+    return shapes
+
+
 def layer_kernel(cfg, *refs):
     fused, nz, ny, rb, own, wide, nf = cfg
     rows_all = 4 * own
     nseg = 8 + 2 * nf
-    gseg = nseg
+    gseg = 8
     refs = list(refs)
 
     def take(count):
@@ -78,7 +92,8 @@
      vt, smix, cmix, slse, clse, act, gbf, dm, dq, dka, dva, dk, dv, ps, pr, ys, yr,
      us, ur, outs, osend, gis, gisend, gms, gmsend, gs, bias, gacc) = take(46)
     if fused:
-        pack, gz, gy, rx, hx, ry, hy, rz = take(8)
+        gz, gy = take(2)
+        sums = {order: take(count) for order, count in SUMS}
     ssem, rsem, xss, xrs, lsem = take(5)
 
     p = lax.axis_index("tensor") // 2
@@ -122,12 +137,32 @@
 
     peers = [core_peer, x_peer]
     if fused:
-        if ny > 1:
-            peers.append(y_peer)
+        peers.append(y_peer)
         peers += [z_peer(k) for k in range(1, nz)]
     barrier = pltpu.get_barrier_semaphore()
     for peer in peers:
         pl.semaphore_signal(barrier, inc=1, device_id=peer, device_id_type=MESH)
+
+    half = pl.ds(pl.multiple_of(p * LANES, LANES), LANES)
+    other_half = pl.ds(pl.multiple_of((1 - p) * LANES, LANES), LANES)
+
+    if fused:
+        own_part = [wqkv_ref[...], wo_ref[...][None], ckv_ref[...], cq_ref[...][None]]
+        own_part.append(co_ref[...][None])
+        at = 0
+        for piece in own_part:
+            wg[at : at + piece.shape[0], z, y, :, half] = piece
+            at += piece.shape[0]
+        for i in range(nf):
+            wg[8 + i, z, y, :, half] = up_ref[:, i * LANES : (i + 1) * LANES]
+            wg[8 + nf + i, z, y, :, half] = dn_ref[:, i * LANES : (i + 1) * LANES]
+        place = (
+            lax.broadcasted_iota(jnp.int32, (rb, wide), 0) + dp_at * rb
+            == lax.broadcasted_iota(jnp.int32, (rb, wide), 1)
+        ).astype(BF16)
+        gz[0] = jnp.zeros((16, wide), BF16)
+        for i in range(6):
+            gz[0, i : i + 1, :] = nn(gain_refs[i][...], place).astype(BF16)
     pl.semaphore_wait(barrier, len(peers))
 
     def spread(src, buf):
@@ -144,77 +179,74 @@
         near.wait_recv()
         return relay
 
-    half = pl.ds(pl.multiple_of(p * LANES, LANES), LANES)
-    other_half = pl.ds(pl.multiple_of((1 - p) * LANES, LANES), LANES)
-
-    def gather_one(lo, hi):
-        return [
-            push(pack.at[lo:hi], wg.at[lo:hi, z, y, :, half], z_peer(k)) for k in range(1, nz)
-        ]
-
-    def gather_two(lo, hi, prior):
-        for cp in prior:
+    def gather(lo, hi, first, last, order):
+        r = slice(first, last)
+        zi, yi, lanes = z, y, half
+        hops = []
+        for axis in order:
+            for cp in hops:
+                cp.wait_recv()
+            part = wg.at[lo:hi, zi, yi, r, lanes]
+            if axis == "x":
+                hops = [push(part, part, x_peer)]
+                lanes = pl.ds(0, 2 * LANES)
+            elif axis == "y":
+                hops = [push(part, part, y_peer)]
+                yi = slice(None)
+            else:
+                hops = [push(part, part, z_peer(k)) for k in range(1, nz)]
+                zi = slice(None)
+            yield
+        for cp in hops:
             cp.wait_recv()
-        if ny == 1:
+        yield
+
+    def gathers(lo, hi, orders):
+        if not fused:
             return []
-        part = wg.at[lo:hi, :, y, :, half]
-        return [push(part, part, y_peer)]
-
-    def gather_three(lo, hi, prior):
-        for cp in prior:
-            cp.wait_recv()
-        part = wg.at[lo:hi, :, :, :, half]
-        return [push(part, part, x_peer)]
+        size = rb // len(orders)
+        return [gather(lo, hi, i * size, (i + 1) * size, o) for i, o in enumerate(orders)]
+
+    def step(parts):
+        for part in parts:
+            next(part)
 
     def weight(s):
         return wg[s].reshape(nz * ny * rb, 2 * LANES)
 
     xin = spread(x_ref, xs)
+    wa = gathers(0, 3, ["zxy", "zyx"])
+    wo_ = gathers(3, 4, ["zxy", "zyx"])
+    wk = gathers(4, 6, ["zxy", "zyx"])
+    wq = gathers(6, 8, ["zxy", "zyx"])
+    wu = gathers(8, 8 + nf, ["xzy"])
+    wd = gathers(8 + nf, nseg, ["xzy"])
     if fused:
-        eye = (
-            lax.broadcasted_iota(jnp.int32, (rb, rb), 0)
-            == lax.broadcasted_iota(jnp.int32, (rb, rb), 1)
-        ).astype(BF16)
-        pack[0:3] = wqkv_ref[...]
-        pack[3] = nt(eye, wo_ref[...]).astype(BF16)
-        pack[4] = cq_ref[...]
-        pack[5:7] = ckv_ref[...]
-        pack[7] = nt(eye, co_ref[...]).astype(BF16)
-        ga = gather_one(0, 3)
-        place = (
-            lax.broadcasted_iota(jnp.int32, (rb, wide), 0) + dp_at * rb
-            == lax.broadcasted_iota(jnp.int32, (rb, wide), 1)
-        ).astype(BF16)
-        gz[0] = jnp.zeros((16, wide), BF16)
-        for i in range(6):
-            gz[0, i : i + 1, :] = nn(gain_refs[i][...], place).astype(BF16)
+        step(wa)
         gcp = [push(gz.at[0], gz.at[k], z_peer(k)) for k in range(1, nz)]
-        for i in range(nf):
-            pack[8 + i] = up_ref[:, i * LANES : (i + 1) * LANES]
-            pack[8 + nf + i] = nt(eye, dn_ref[i * LANES : (i + 1) * LANES, :]).astype(BF16)
-        wg[:, z, y, :, half] = pack[...]
+        step(wo_)
+        step(wk)
+        step(wq)
+        step(wa)
         for cp in gcp:
             cp.wait_recv()
         total = gz[0].astype(F32)
         for k in range(1, nz):
             total = total + gz[k].astype(F32)
-        if ny > 1:
-            gy[0] = total.astype(BF16)
-            gcp = push(gy.at[0], gy.at[1], y_peer)
-            gcp.wait_recv()
-            total = total + gy[1].astype(F32)
+        gy[0] = total.astype(BF16)
+        gcp = push(gy.at[0], gy.at[1], y_peer)
+        step(wo_)
+        relay = settle(xin, xs)
+        gcp.wait_recv()
+        total = total + gy[1].astype(F32)
         gains[...] = total
-        ga = gather_two(0, 3, ga)
-        go = gather_one(3, 4)
-        gb = gather_one(4, 8)
+        step(wu)
+        step(wd)
     else:
         wcp = local(wfull_ref, wg)
         gains[...] = gfull_ref[...]
+        relay = settle(xin, xs)
         wcp.wait()
-    min_ = spread(m_ref, ms)
-    cin = spread(c_ref, cs)
-
-    relay = settle(xin, xs)
     relay.wait_recv()
 
     sub = min(64, own)
@@ -228,14 +260,11 @@
         return 0
 
     lax.fori_loop(0, 4 * per, norm_rows, 0)
-
-    if fused:
-        ga = gather_three(0, 3, ga)
-        go = gather_two(3, 4, go)
-        gb = gather_two(4, 8, gb)
-        gc = gather_one(8, nseg)
-        for cp in ga:
-            cp.wait_recv()
+    step(wa)
+    step(wo_)
+    step(wk)
+    min_ = spread(m_ref, ms)
+    step(wa)
 
     def put_pairs(buf, r, value):
         v = value.astype(BF16)
@@ -264,10 +293,6 @@
 
     lax.fori_loop(0, 4, project, 0)
 
-    if fused:
-        go = gather_three(3, 4, go)
-        gb = gather_three(4, 8, gb)
-        gc = gather_two(8, nseg, gc)
 
     def only(value, u):
         lane = lax.broadcasted_iota(jnp.int32, value.shape, 1)
@@ -326,17 +351,19 @@
     for j in range(4):
         r = rows(j)
         attend(qs, ks, vt, smix, slse, r, own * (j + 1), True)
-        if fused and j == 0:
-            for cp in go:
-                cp.wait_recv()
+        if j == 0:
+            step(wo_)
+            step(wu)
         send_sum(0, j, nt(pairs(smix, r), weight(3)))
         if j == 1:
+            step(wk)
+            step(wq)
+        if j == 2:
             mrelay = settle(min_, ms)
-
-    if fused:
-        for cp in gb:
-            cp.wait_recv()
-        gc = gather_three(8, nseg, gc)
+            step(wd)
+    step(wk)
+    step(wq)
+    cin = spread(c_ref, cs)
     mrelay.wait_recv()
 
     key_at = lax.broadcasted_iota(jnp.int32, (rows_all, LANES), 0)
@@ -345,13 +372,14 @@
     def project_cross(j, _):
         r = rows(j)
         rowsv = ms[r, :]
-        put_pairs(cks, r, nn(rowsv, weight(5)))
-        val = nn(rowsv, weight(6))
+        put_pairs(cks, r, nn(rowsv, weight(4)))
+        val = nn(rowsv, weight(5))
         put_pairs(cvs, r, val)
         put_transposed(vt, r, val.astype(BF16).astype(F32))
         return 0
 
     lax.fori_loop(0, 4, project_cross, 0)
+    step(wq)
 
     def second(j, _):
         exchange(0, j).wait_recv()
@@ -367,7 +395,7 @@
 
         lax.fori_loop(0, per, part, 0)
         r = rows(j)
-        put_pairs(cqs, r, nn(n2[r, :], weight(4)).astype(BF16) * jnp.asarray(scale, BF16))
+        put_pairs(cqs, r, nn(n2[r, :], weight(6)).astype(BF16) * jnp.asarray(scale, BF16))
         return 0
 
     lax.fori_loop(0, 4, second, 0)
@@ -378,12 +406,16 @@
         send_sum(1, j, nt(pairs(cmix, r), weight(7)))
         return 0
 
-    lax.fori_loop(0, 4, cross_block, 0)
+    cross_block(0, 0)
+    step(wu)
+    cross_block(1, 0)
+    cross_block(2, 0)
+    step(wd)
+    step(wu)
+    cross_block(3, 0)
     crelay = settle(cin, cs)
+    step(wd)
     crelay.wait_recv()
-    if fused:
-        for cp in gc:
-            cp.wait_recv()
 
     limit = tl_ref[p]
 
@@ -446,51 +478,90 @@
     def plane(buf, s):
         return lambda: buf[s]
 
-    weight_grads(gb16, [(8 + nf + s, plane(act, s)) for s in range(nf)])
-    weight_grads(n3, [(8 + s, plane(gbf, s)) for s in range(nf)])
-
-    def reduce_one(lo, hi):
-        return push(gs.at[lo:hi, :, :, :, other_half], rx.at[lo:hi], x_peer)
-
-    def reduce_two(lo, hi, prior):
-        prior.wait_recv()
-        def one(s, _):
-            mine = gs[s, :, :, :, half].astype(F32)
-            hx[s] = (mine + rx[s].astype(F32)).astype(BF16)
-            return 0
-        lax.fori_loop(lo, hi, one, 0)
-        if ny == 1:
-            return None
-        return push(hx.at[lo:hi, :, 1 - y], ry.at[lo:hi], y_peer)
-
-    def reduce_three(lo, hi, prior):
-        if prior is not None:
-            prior.wait_recv()
-        def one(s, _):
-            v = hx[s, :, y].astype(F32)
-            if ny > 1:
-                v = v + ry[s].astype(F32)
-            hy[s] = v.astype(BF16)
-            return 0
-        lax.fori_loop(lo, hi, one, 0)
-        return [
-            push(hy.at[lo:hi, (z + k) % nz], rz.at[k - 1, lo:hi], z_peer(k))
-            for k in range(1, nz)
-        ]
-
-    def reduce_done(lo, hi, prior):
-        for cp in prior:
-            cp.wait_recv()
-        def one(s, _):
-            v = hy[s, z].astype(F32)
-            for k in range(1, nz):
-                v = v + rz[k - 1, s].astype(F32)
-            gw_ref[s] = v
-            return 0
-        lax.fori_loop(lo, hi, one, 0)
-
-    if fused:
-        rf = reduce_one(8, nseg)
+    rh = rb // 2
+
+    def reduce_part(lo, hi, base, first, last, order):
+        r = slice(first, last)
+        bufs = list(sums[order])
+        gone = []
+
+        def at(buf, s, zsel, ysel, lsel):
+            index = [s]
+            if "z" not in gone:
+                index.append(zsel)
+            if "y" not in gone:
+                index.append(ysel)
+            index += [slice(None) if buf is not gs else r, lsel]
+            return tuple(index)
+
+        every_one = slice(None)
+        cur, shift = gs, 0
+        for hop, axis in enumerate(order):
+            span = slice(lo - shift, hi - shift)
+            land = bufs.pop(0)
+            to = slice(lo - base, hi - base)
+            lanes = every_one if "x" in gone else slice(0, 2 * LANES)
+            pick = {"z": every_one, "y": every_one, "x": lanes}
+            here = dict(pick)
+            if axis == "x":
+                pick["x"], here["x"] = other_half, half
+                sends = [(pick, land.at[to], x_peer)]
+            elif axis == "y":
+                pick["y"], here["y"] = 1 - y, y
+                sends = [(pick, land.at[to], y_peer)]
+            else:
+                here["z"] = z
+                sends = [
+                    (dict(pick, z=(z + k) % nz), land.at[k - 1, to], z_peer(k))
+                    for k in range(1, nz)
+                ]
+            cps = [
+                push(cur.at[at(cur, span, sel["z"], sel["y"], sel["x"])], dst, peer)
+                for sel, dst, peer in sends
+            ]
+            yield
+            for cp in cps:
+                cp.wait_recv()
+            done = hop == 2
+            acc = None if done else bufs.pop(0)
+
+            def add(s, _):
+                v = cur[at(cur, s - shift, here["z"], here["y"], here["x"])].astype(F32)
+                if axis == "z":
+                    for k in range(1, nz):
+                        v = v + land[k - 1, s - base].astype(F32)
+                else:
+                    v = v + land[s - base].astype(F32)
+                if done:
+                    gw_ref[s, r] = v
+                else:
+                    acc[s - base] = v.astype(BF16)
+                return 0
+
+            lax.fori_loop(lo, hi, add, 0)
+            gone.append(axis)
+            cur, shift = acc, base
+        yield
+
+    def reduces(lo, hi, halves):
+        if not fused:
+            return []
+        if halves:
+            return [
+                reduce_part(lo, hi, 0, 0, rh, "xyz"),
+                reduce_part(lo, hi, 0, rh, rb, "yxz"),
+            ]
+        return [reduce_part(lo, hi, 9, 0, rb, "yzx")]
+
+    rfu = reduces(9, 9 + nf, False)
+    rfd = reduces(9 + nf, nseg + 1, False)
+    rc = reduces(3, 8, True)
+    rt = reduces(0, 3, True)
+    rg = reduces(gseg, gseg + 1, True)
+    weight_grads(gb16, [(9 + nf + s, plane(act, s)) for s in range(nf)])
+    step(rfd)
+    weight_grads(n3, [(9 + s, plane(gbf, s)) for s in range(nf)])
+    step(rfu)
 
     def finish_rows(k, dst):
         def part(i, _):
@@ -526,8 +597,6 @@
 
     lax.fori_loop(0, 4, back_three, 0)
 
-    if fused:
-        rf = reduce_two(8, nseg, rf)
 
     sel_row = lax.broadcasted_iota(jnp.int32, (8, LANES), 0)
     sel_lane = lax.broadcasted_iota(jnp.int32, (8, LANES), 1)
@@ -579,19 +648,19 @@
         r = rows(j)
         put_pairs(dm, r, nn(gb16[r, :], weight(7)))
         attend_back(cqs, cks, vt, cvs, cmix, clse, r, rows_all, False)
-        send_sum(3, j, nt(pairs(dq, r), weight(4)))
+        send_sum(3, j, nt(pairs(dq, r), weight(6)))
         return 0
 
-    lax.fori_loop(0, 4, cross_back, 0)
-    if fused:
-        rf = reduce_three(8, nseg, rf)
+    lax.fori_loop(0, 2, cross_back, 0)
+    step(rfd)
+    lax.fori_loop(2, 4, cross_back, 0)
 
     def cross_back_keys(j, _):
         r = rows(j)
         for pp in range(2):
             dk[pp, r, :] = dka[pp, r, :].astype(BF16)
             dv[pp, r, :] = dva[pp, r, :].astype(BF16)
-        val = nt(pairs(dk, r), weight(5)) + nt(pairs(dv, r), weight(6))
+        val = nt(pairs(dk, r), weight(4)) + nt(pairs(dv, r), weight(5))
         us[r, :] = val.astype(BF16)
         return 0
 
@@ -600,8 +669,8 @@
         push(us.at[rows(2 * k + 1 - c)], ur.at[k], core_peer) for k in range(2)
     ]
     weight_grads(gb16, [(7, whole(cmix))])
-    weight_grads(n2, [(4, whole(dq))])
-    weight_grads(ms, [(5, whole(dk)), (6, whole(dv))])
+    weight_grads(n2, [(6, whole(dq))])
+    weight_grads(ms, [(4, whole(dk)), (5, whole(dv))])
 
     def memory_rows(k, dst):
         def part(i, _):
@@ -635,9 +704,8 @@
 
     lax.fori_loop(0, 4, back_two, 0)
     weight_grads(gb16, [(3, whole(smix))])
-    if fused:
-        reduce_done(8, nseg, rf)
-        rc = reduce_one(3, 8)
+    step(rfu)
+    step(rc)
 
     transpose_keys(ks)
     dka[...] = jnp.zeros_like(dka)
@@ -651,15 +719,17 @@
             dv[pp, r, :] = dva[pp, r, :].astype(BF16)
         val = nt(pairs(dq, r), weight(0)) + nt(pairs(dk, r), weight(1))
         send_sum(4, j, val + nt(pairs(dv, r), weight(2)))
-        if fused and j == 3:
-            rc = reduce_two(3, 8, rc)
-        if fused and j == 2:
-            rc = reduce_three(3, 8, rc)
+        if j == 3:
+            step(rfd)
+        if j == 2:
+            step(rfu)
+            step(rc)
+        if j == 1:
+            step(rfd)
 
     weight_grads(n1, [(0, whole(dq)), (1, whole(dk)), (2, whole(dv))])
-    if fused:
-        rt = reduce_one(0, 3)
-        reduce_done(3, 8, rc)
+    step(rt)
+    step(rc)
 
     def back_one(k, j, dst):
         exchange(4, j).wait_recv()
@@ -690,27 +760,42 @@
     columns = spread_rows.T.astype(BF16)
     gs[gseg] = jnp.concatenate([columns, columns], axis=1).reshape(nz, ny, rb, 2 * LANES)
 
-    if fused:
-        rg = reduce_one(gseg, gseg + 1)
-        rt = reduce_two(0, 3, rt)
-        rg = reduce_two(gseg, gseg + 1, rg)
-        rt = reduce_three(0, 3, rt)
-        rg = reduce_three(gseg, gseg + 1, rg)
-        reduce_done(0, 3, rt)
-        reduce_done(gseg, gseg + 1, rg)
-    else:
-        last = [local(gs, gw_ref)]
+    step(rg)
+    step(rt)
+    step(rfu)
+    step(rg)
+    step(rc)
+    step(rt)
+    step(rg)
+    step(rt)
+    step(rg)
+    last = [] if fused else [local(gs, gw_ref)]
 
     ocp.wait_recv()
     mcp.wait_recv()
     icp.wait_recv()
     finals = [local(outs, out_ref), local(gms, gm_ref), local(gis, gi_ref)]
-    if not fused:
-        finals += last
-    for cp in finals:
+    for cp in finals + last:
         cp.wait()
     for cp in sent:
         cp.wait_send()
+
+
+def unpack_kernel(nf, o_ref, gi_ref, gm_ref, gw_ref, *outs):
+    outs[0][...] = o_ref[...]
+    outs[1][...] = gi_ref[...].astype(F32)
+    outs[2][...] = gm_ref[...].astype(F32)
+    outs[3][...] = gw_ref[0:3]
+    outs[4][...] = gw_ref[3]
+    outs[5][...] = gw_ref[6]
+    outs[6][...] = gw_ref[4:6]
+    outs[7][...] = gw_ref[7]
+    for i in range(nf):
+        outs[8][:, i * LANES : (i + 1) * LANES] = gw_ref[9 + i]
+        outs[9][:, i * LANES : (i + 1) * LANES] = gw_ref[9 + nf + i]
+    vectors = gw_ref[8].T
+    for i in range(6):
+        outs[10 + i][...] = vectors[i : i + 1]
 
 
 def body(ndp, inputs, memory, tgt_len, src_len, cotangent, w_qkv, w_out, cross_query, cross_kv,
@@ -720,11 +805,9 @@
     nf = ffn_up.shape[1] // LANES
     nseg = 8 + 2 * nf
     rows_all = 4 * own
-    fused = rb % 16 == 0
+    fused = rb % 32 == 0 and ndp % 2 == 0
     if fused:
-        ny = 2 if ndp % 2 == 0 else 1
-        nz = ndp // ny
-        block = rb
+        ny, nz, block = 2, ndp // 2, rb
     else:
         ny, nz, block = 1, 1, wide
     cfg = (fused, nz, ny, block, own, wide, nf)
@@ -735,12 +818,12 @@
     operands = [inputs, memory, cotangent, tgt_len, src_len]
     specs = [any_spec] * 3 + [smem] * 2
     if fused:
-        weights = [w_qkv, w_out, cross_query, cross_kv, cross_out, ffn_up, ffn_down]
+        weights = [w_qkv, w_out.T, cross_query, cross_kv, cross_out.T, ffn_up, ffn_down.T]
         weights += [g[None, :] for g in gain_list]
         operands += weights
         specs += [vmem] * len(weights)
     else:
-        pieces = [w_qkv, w_out.T[None], cross_query[None], cross_kv, cross_out.T[None]]
+        pieces = [w_qkv, w_out.T[None], cross_kv, cross_query[None], cross_out.T[None]]
         pieces += [ffn_up.reshape(rb, nf, LANES).swapaxes(0, 1)]
         pieces += [ffn_down.reshape(nf, LANES, rb).swapaxes(1, 2)]
         packed = lax.all_gather(jnp.concatenate(pieces, axis=0), "dp", axis=1, tiled=True)
@@ -770,14 +853,13 @@
         bf(nseg + 1, nz, ny, block, 2 * LANES), fl(rows_all, LANES), fl(8, wide),
     ]
     if fused:
-        scratch += [
-            bf(nseg, block, LANES), bf(nz, 16, wide), bf(2, 16, wide),
-            bf(nseg + 1, nz, ny, block, LANES), bf(nseg + 1, nz, ny, block, LANES),
-            bf(nseg + 1, nz, block, LANES), bf(nseg + 1, nz, block, LANES),
-            bf(max(nz - 1, 1), nseg + 1, block, LANES),
-        ]
+        small = block // 2
+        scratch += [bf(nz, 16, wide), bf(2, 16, wide)]
+        for order, _count in SUMS:
+            segs, size = (nseg - 8, block) if order == "yzx" else (9, small)
+            scratch += [bf(*shape) for shape in sum_shapes(order, segs, nz, ny, size)]
     dma = pltpu.SemaphoreType.DMA
-    scratch += [dma((96,)), dma((96,)), dma((20,)), dma((20,)), dma((12,))]
+    scratch += [dma((160,)), dma((160,)), dma((20,)), dma((20,)), dma((12,))]
 
     if fused:
         grads_shape = jax.ShapeDtypeStruct((nseg + 1, block, LANES), F32)
@@ -807,27 +889,22 @@
         keep = keep + lax.ppermute(give, "tensor", [(i, (i + 2) % 4) for i in range(4)])
         grads = lax.psum_scatter(keep, "dp", scatter_dimension=1, tiled=True)
 
-    def merge(blocks):
-        return jnp.swapaxes(blocks, 0, 1).reshape(blocks.shape[1], -1)
-
-    gain_grads = grads[nseg][:, :6].T
+    shapes = [
+        (inputs.shape, BF16), (inputs.shape, F32), (memory.shape, F32),
+        (w_qkv.shape, F32), (w_out.shape[::-1], F32), (cross_query.shape, F32),
+        (cross_kv.shape, F32), (cross_out.shape[::-1], F32), (ffn_up.shape, F32),
+        (ffn_down.shape[::-1], F32),
+    ] + [((1, rb), F32)] * 6
+    got = pl.pallas_call(
+        functools.partial(unpack_kernel, nf),
+        out_shape=[jax.ShapeDtypeStruct(*s) for s in shapes],
+        in_specs=[vmem] * 4,
+        out_specs=[vmem] * len(shapes),
+        name="unpack",
+    )(output, grad_in, grad_mem, grads)
     return (
-        output,
-        grad_in.astype(F32),
-        grad_mem.astype(F32),
-        grads[0:3],
-        grads[3].T,
-        grads[4],
-        grads[5:7],
-        grads[7].T,
-        merge(grads[8 : 8 + nf]),
-        merge(grads[8 + nf : nseg]).T,
-        gain_grads[0],
-        gain_grads[1],
-        gain_grads[2],
-        gain_grads[3],
-        gain_grads[4],
-        gain_grads[5],
+        *got[:4], got[4].T, got[5], got[6], got[7].T, got[8], got[9].T,
+        *[g[0] for g in got[10:]],
     )
 
 

time: 218 us -> 169 us (0.78)
  Pallas kernels: 203 us -> 168 us
  local copies, waits for them, and re-layouts: 11.4 us -> 0 us
  other arithmetic: 2.2 us -> 0 us
    pallas_call x1, Pallas kernels: 203 us -> 165 us  [body(): pl.pallas_call(functools.partial(layer_kernel, cfg), out_shape=(act_shape...]
    unnamed x13 -> x0, local copies, waits for them, and re-layouts: 5.45 us -> none
    slice x3 -> x0, local copies, waits for them, and re-layouts: 3.81 us -> none  [the longest x1 1.54 us: body(): grads[0:3]]
    pallas_call x0 -> x1, Pallas kernels: none -> 3.3 us  [body(): pl.pallas_call(functools.partial(unpack_kernel, nf), out_shape=[jax.Shape...]
    convert_element_type x2 -> x0, other arithmetic: 2.2 us -> none  [the longest x1 1.1 us: body(): grad_in.astype(F32)]
where the time goes in v2:
time: 169 us
  Pallas kernels  168 us (99%)
    pallas_call x1, Pallas kernels, body(): pl.pallas_call(functools.partial(layer_kernel, cfg), out_shape=(act_shape...  165 us

profile of v2, /device:TPU:0, one launch (start us, length us, event | category | flops | bytes accessed | tf_op | source)
XLA Modules:
  0.0 169.2 jit_solution(5067123677502359940)
XLA Ops:
  0.7 165.0 %layer.1 = (bf16[2,256,512]{2,1,0:T(8,128)(2,1)}, bf16[2,256,512]{2,1,0:T(8,128)(2,1)}, bf16[2,256,512]{2,1,0:T(8,128)(2,1)}, f32[17,64,128]{2,1,0:T(8,128)}) custom-call(bf16[2,256,512]{2,1,0:T(8,128)(2,1)} %refs_0_.1, bf16[2,256,512]{2,1,0:T(8,128)(2,1)} %refs_1_.1, bf16[2,256,512]{2,1,0:T(8,128)(2,1)} %refs_2_.1, s32[2]{0:T(128)} %refs_3_.1, s32[2]{0:T(128)} %refs_4_.1, ...), custom_call_target="tpu_custom_call" | custom-call | tf_op jit(solution)/shard_map/layer/pallas_call | solution.py:871
  165.7 3.3 %unpack.1 = (bf16[2,256,512]{2,1,0:T(8,128)(2,1)}, f32[2,256,512]{2,1,0:T(8,128)}, f32[2,256,512]{2,1,0:T(8,128)}, f32[3,64,128]{2,1,0:T(8,128)}, f32[64,128]{1,...) custom-call(bf16[2,256,512]{2,1,0:T(8,128)(2,1)} %get-tuple-element., ...), custom_call_target="tpu_custom_call" | custom-call | tf_op jit(solution)/shard_map/unpack/pallas_call | solution.py:898
